TPU v7x, 256 devices: a whole 4x4x8 slice. The times are simulated.
256 devices in a mesh: seq: 16 (over z, core), fsdp: 16 (over x, y).
Axes of the slice: x: 4, y: 4, z: 8, core: 2. Of those that a mesh axis runs over, the one named last changes fastest.
Arguments:
- inputs: bfloat16 [16, 2048, 2304], P('fsdp', 'seq'), may hold values from -6 to 6
- queries: bfloat16 [16, 2048, 2048], P('fsdp', 'seq'), may hold values from -96 to 96
- w_kv: bfloat16 [2304, 2048], P('fsdp'), may hold values from -0.125 to 0.125
- doc_lengths: int32 [16, 8], P('fsdp'), may hold values from 1 to 1536, 2048 in all within a row
- grad_out: bfloat16 [16, 2048, 2048], P('fsdp', 'seq'), may hold values from -6 to 6
Outputs:
- attn_out: bfloat16 [16, 2048, 2048], P('fsdp', 'seq')
- grad_inputs: bfloat16 [16, 2048, 2304], P('fsdp', 'seq')
- grad_weights: float32 [2304, 2048], P('fsdp', 'seq')
Inputs may be any that keep to these rules, and one draw needn't show every extreme that they name: `doc_lengths`: each row lists the lengths of the 8 documents packed in order into one sequence; a row sums to 2048 and its longest document has 1536 tokens.
All inputs are finite; a program needn't handle non-finite values.
Results may differ from a plain program's by a relative error of at most 0.03.
Values may be sent and summed in bfloat16 or wider, within the bound.
A program may use at most 128 MiB of HBM per device.

v0:
```python
import jax
import jax.numpy as jnp
from jax import lax
from jax.sharding import PartitionSpec as P

QH = 16
KVH = 8
HD = 128
WIN = 1024
G = 2


SOFT_CAP = 50.0
QUERY_SCALE = 1.0 / 12.0
ROPE_BASE = 10000.0


def from_behind(value, axis, steps):
    count = lax.axis_size(axis)
    first, last = (max(0, -steps), min(count, count - steps))
    return lax.ppermute(value, axis, [(source, source + steps) for source in range(first, last)])


def doc_layout(lengths, places):
    doc_ends = jnp.cumsum(lengths)
    doc_ended = doc_ends[None, :] <= places[:, None]
    doc_index = jnp.sum(doc_ended.astype(jnp.int32), axis=1)
    before = jnp.sum(jnp.where(doc_ended, lengths[None, :], 0), axis=1)
    return (doc_index, places - before)


def rotate(values, places, direction):
    half_dim = values.shape[-1] // 2
    exponent = jnp.arange(half_dim, dtype=jnp.float32) * (2.0 / values.shape[-1])
    inverse_rate = jnp.power(ROPE_BASE, -exponent)
    angles = places.astype(jnp.float32)[:, None] * inverse_rate[None, :]
    cosine = jnp.cos(angles)[:, None, :]
    sine_part = direction * jnp.sin(angles)[:, None, :]
    first_half = values[..., :half_dim]
    second_half = values[..., half_dim:]
    return jnp.concatenate(
        [
            first_half * cosine - second_half * sine_part,
            second_half * cosine + first_half * sine_part,
        ],
        axis=-1,
    )


def attend(earlier, query_rows, cotangent, window, allowed):
    row_count = query_rows.shape[0]
    used_rows = (earlier + 1) * row_count
    half_kv = KVH * HD
    pair_width = 2 * G * HD

    def one_pair(pair_index, state_now):
        out_acc, key_acc, value_acc = state_now
        q_part = lax.dynamic_slice_in_dim(
            query_rows, pair_index * pair_width, pair_width, 1
        ).reshape(row_count, 2, G, HD)
        d_part = lax.dynamic_slice_in_dim(
            cotangent, pair_index * pair_width, pair_width, 1
        ).reshape(row_count, 2, G, HD)
        k_part = lax.dynamic_slice_in_dim(window, pair_index * 2 * HD, 2 * HD, 1).reshape(
            used_rows, 2, HD
        )
        v_part = lax.dynamic_slice_in_dim(window, half_kv + pair_index * 2 * HD, 2 * HD, 1).reshape(
            used_rows, 2, HD
        )
        scores = (
            jnp.einsum("tkgd,nkd->kgtn", q_part, k_part, preferred_element_type=jnp.float32)
            * QUERY_SCALE
        )
        squashed = jnp.tanh(scores / SOFT_CAP)
        weights = jnp.where(allowed[None, None], jnp.exp(SOFT_CAP * squashed), 0.0)
        probs = weights / jnp.sum(weights, axis=-1, keepdims=True)
        rounded = probs.astype(jnp.bfloat16)
        attended = jnp.einsum(
            "kgtn,nkd->tkgd", rounded, v_part, preferred_element_type=jnp.float32
        ).astype(jnp.bfloat16)
        delta_row = jnp.einsum(
            "tkgd,tkgd->kgt", d_part, attended, preferred_element_type=jnp.float32
        )
        dprob = jnp.einsum("tkgd,nkd->kgtn", d_part, v_part, preferred_element_type=jnp.float32)
        dscore = (probs * (dprob - delta_row[..., None]) * (1.0 - squashed * squashed)).astype(
            jnp.bfloat16
        )
        key_grad = (
            jnp.einsum("kgtn,tkgd->nkd", dscore, q_part, preferred_element_type=jnp.float32)
            * QUERY_SCALE
        )
        value_grad = jnp.einsum(
            "kgtn,tkgd->nkd", rounded, d_part, preferred_element_type=jnp.float32
        )
        out_acc = lax.dynamic_update_slice_in_dim(
            out_acc, attended.reshape(row_count, pair_width), pair_index * pair_width, 1
        )
        key_acc = lax.dynamic_update_slice_in_dim(
            key_acc, key_grad.reshape(used_rows, 2 * HD), pair_index * 2 * HD, 1
        )
        value_acc = lax.dynamic_update_slice_in_dim(
            value_acc, value_grad.reshape(used_rows, 2 * HD), pair_index * 2 * HD, 1
        )
        return (out_acc, key_acc, value_acc)

    initial = (
        jnp.zeros((row_count, QH * HD), jnp.bfloat16),
        jnp.zeros((used_rows, half_kv), jnp.float32),
        jnp.zeros((used_rows, half_kv), jnp.float32),
    )
    out_rows, key_grads, value_grads = lax.fori_loop(0, KVH // 2, one_pair, initial)
    return (out_rows, key_grads, value_grads)


def on_device(inputs, queries, w_kv, doc_lengths, grad_out):
    tokens = inputs[0]
    query_rows = queries[0]
    cotangent = grad_out[0]
    lengths = doc_lengths[0]
    row_count = tokens.shape[0]
    seq_count = lax.axis_size("seq")
    shard_index = lax.axis_index("seq")
    reach_blocks = min((WIN + row_count - 2) // row_count, seq_count - 1)
    half_kv = KVH * HD
    weight_full = lax.all_gather(w_kv, "fsdp", axis=0, tiled=True)
    projected = jnp.dot(tokens, weight_full, preferred_element_type=jnp.float32)
    places = shard_index * row_count + jnp.arange(row_count, dtype=jnp.int32)
    doc_index, within = doc_layout(lengths, places)
    own_keys = rotate(projected[:, :half_kv].reshape(row_count, KVH, HD), within, 1.0).reshape(
        row_count, half_kv
    )
    own_block = jnp.concatenate([own_keys, projected[:, half_kv:]], axis=1).astype(jnp.bfloat16)
    received = [own_block]
    for offset in range(1, reach_blocks + 1):
        received.append(from_behind(own_block, "seq", offset))
    window = jnp.concatenate(received[::-1], axis=0)
    key_places = (shard_index - reach_blocks) * row_count + jnp.arange(
        (reach_blocks + 1) * row_count, dtype=jnp.int32
    )
    key_doc, ignored = doc_layout(lengths, key_places)
    distance = places[:, None] - key_places[None, :]
    allowed = (
        (key_places[None, :] >= 0)
        & (doc_index[:, None] == key_doc[None, :])
        & (distance >= 0)
        & (distance <= WIN - 1)
    )
    out_rows, key_grads, value_grads = attend(reach_blocks, query_rows, cotangent, window, allowed)
    split_at = reach_blocks * row_count
    remote = jnp.concatenate(
        [key_grads[:split_at].astype(jnp.bfloat16), value_grads[:split_at].astype(jnp.bfloat16)],
        axis=1,
    )
    remote = remote.reshape(reach_blocks, row_count, 2 * half_kv)
    summed = jnp.concatenate([key_grads[split_at:], value_grads[split_at:]], axis=1)
    for offset in range(1, reach_blocks + 1):
        arrived = from_behind(remote[reach_blocks - offset], "seq", -offset)
        summed = summed + arrived.astype(jnp.float32)
    key_total = rotate(summed[:, :half_kv].reshape(row_count, KVH, HD), within, -1.0).reshape(
        row_count, half_kv
    )
    grad_kv = jnp.concatenate([key_total, summed[:, half_kv:]], axis=1).astype(jnp.bfloat16)
    grad_rows = jnp.dot(grad_kv, weight_full.T, preferred_element_type=jnp.float32).astype(
        jnp.bfloat16
    )
    shared = lax.psum_scatter(
        lax.dot_general(
            tokens, grad_kv, (((0,), (0,)), ((), ())), preferred_element_type=jnp.float32
        ).astype(jnp.bfloat16),
        "fsdp",
        scatter_dimension=0,
        tiled=True,
    )
    finished = lax.psum_scatter(shared, "seq", scatter_dimension=1, tiled=True).astype(jnp.float32)
    return (out_rows[None], grad_rows[None], finished)


def solution(mesh):
    in_specs = (
        P("fsdp", "seq", None),
        P("fsdp", "seq", None),
        P("fsdp", None),
        P("fsdp", None),
        P("fsdp", "seq", None),
    )
    out_specs = (P("fsdp", "seq", None), P("fsdp", "seq", None), P("fsdp", "seq"))
    return jax.shard_map(
        on_device, mesh=mesh, in_specs=in_specs, out_specs=out_specs, check_vma=False
    )
```

profile of v0, /device:TPU:192, one launch (start us, length us, event | category | flops | bytes accessed | tf_op | source)
XLA Modules:
  0.0 716.8 jit_solution(4703402251227408415)
XLA Ops:
  11.6 80.4 %all-gather.2.cloned.1.call-done = bf16[2304,2048]{1,0:T(8,128)(2,1)} async-done(((bf16[144,2048]{1,0:T(8,128)(2,1)}), bf16[2304,2048]{1,0:T(8,128)(2,1)}) %all-gather.2.cloned.1.call-update) | async-done | bytes 9437200 | tf_op jit(solution)/shard_map/all_gather | solution.py:125
  92.0 5.1 fusion.32
  103.8 1.9 collective-permute-start.7
  105.7 2.6 collective-permute-start.6
  108.2 66.7 %collective-permute-done = bf16[128,2048]{1,0:T(8,128)(2,1)} collective-permute-done((bf16[128,2048]{1,0:T(8,128)(2,1)S(1)}, bf16[128,2048]{1,0:T(8,128)(2,1)}, u32[]{:S(2)}, u32[]{:S(2)}) %collective-permute-start) | collective-permute-done | bytes 524320 | tf_op jit(solution)/shard_map/ppermute | solution.py:21
  176.2 1.9 constant_dynamic-update-slice_fusion.11
  178.2 5.8 collective-permute-done.1
  185.3 1.9 constant_dynamic-update-slice_fusion.10
  187.2 1.9 collective-permute-start.5
  189.1 1.9 constant_dynamic-update-slice_fusion.9
  191.0 33.3 %collective-permute-done.3 = bf16[128,2048]{1,0:T(8,128)(2,1)S(1)} collective-permute-done((bf16[128,2048]{1,0:T(8,128)(2,1)S(1)}, bf16[128,2048]{1,0:T(8,128)(2,1)S(1)}, u32[]{:S(2)}, u32[]{:S(2)}) %collective-permute-start.3) | collective-permute-done | bytes 524320 | tf_op jit(solution)/shard_map/ppermute | solution.py:21
  225.1 18.2 %collective-permute-done.4 = bf16[128,2048]{1,0:T(8,128)(2,1)S(1)} collective-permute-done((bf16[128,2048]{1,0:T(8,128)(2,1)S(1)}, bf16[128,2048]{1,0:T(8,128)(2,1)S(1)}, u32[]{:S(2)}, u32[]{:S(2)}) %collective-permute-start.4) | collective-permute-done | bytes 524320 | tf_op jit(solution)/shard_map/ppermute | solution.py:21
  247.5 6.7 copy.70
  255.1 2.5 broadcast.142.clone
  257.6 2.4 broadcast.142
  260.0 72.9 %while.20 = (s32[]{:T(128)}, bf16[128,2048]{1,0:T(8,128)(2,1)}, f32[1152,1024]{0,1:T(8,128)}, f32[1152,1024]{0,1:T(8,128)}, bf16[1152,2048]{0,1:T(8,128)(2,1)}, ...) while((s32[]{:T(128)}, bf16[128,2048]{1,0:T(8,128)(2,1)}, ...), condition=%wide.region_6.7_spmd.clone, body=%wide.region_4.6_spmd.clone.sunk | while | flops 766655488 | bytes 39024268 | solution.py:111
  260.8 1.9 fusion.82
  268.2 2.2 fusion.85
  270.4 3.1 fusion.87
  279.1 1.9 fusion.82
  286.4 2.2 fusion.85
  288.6 3.1 fusion.87
  297.3 1.9 fusion.82
  304.6 2.2 fusion.85
  306.8 3.1 fusion.87
  313.0 1.8 constant_dynamic-update-slice_fusion.15
  315.5 1.9 fusion.82
  322.9 2.2 fusion.85
  325.1 3.1 fusion.87
  333.0 2.5 slice.167
  335.5 2.5 slice.168
  338.0 2.8 fusion.35
  340.8 11.7 %collective-permute-start.8 = (bf16[128,2048]{0,1:T(8,128)(2,1)S(1)}, bf16[128,2048]{0,1:T(8,128)(2,1)S(1)}, u32[]{:S(2)}, u32[]{:S(2)}) collective-permute-start(bf16[128,2048]{0,1:T(8,128)(2,1)S(1)} %get-tuple-element.348), channel_id=1, source_target_pairs={{16,0},{32,16},{48,32},{64,48},{80,64},{96,80},{112,96},{128,112},... | collective-permute-start | bytes 1572872 | tf_op jit(solution)/shard_map/ppermute | solution.py:21
  352.5 18.7 %collective-permute-start.9 = (bf16[128,2048]{0,1:T(8,128)(2,1)S(1)}, bf16[128,2048]{0,1:T(8,128)(2,1)S(1)}, u32[]{:S(2)}, u32[]{:S(2)}) collective-permute-start(bf16[128,2048]{0,1:T(8,128)(2,1)S(1)} %get-tuple-element.349), channel_id=1, source_target_pairs={{32,0},{48,16},{64,32},{80,48},{96,64},{112,80},{128,96},{144,112}... | collective-permute-start | bytes 1572872 | tf_op jit(solution)/shard_map/ppermute | solution.py:21
  371.2 6.9 collective-permute-start.10
  378.0 1.8 collective-permute-start.11
  381.2 4.8 collective-permute-start.13
  386.0 59.2 %collective-permute-done.9 = bf16[128,2048]{0,1:T(8,128)(2,1)S(1)} collective-permute-done((bf16[128,2048]{0,1:T(8,128)(2,1)S(1)}, bf16[128,2048]{0,1:T(8,128)(2,1)S(1)}, u32[]{:S(2)}, u32[]{:S(2)}) %collective-permute-start.9) | collective-permute-done | bytes 524320 | tf_op jit(solution)/shard_map/ppermute | solution.py:21
  446.5 9.9 %collective-permute-done.10 = bf16[128,2048]{0,1:T(8,128)(2,1)S(1)} collective-permute-done((bf16[128,2048]{0,1:T(8,128)(2,1)S(1)}, bf16[128,2048]{0,1:T(8,128)(2,1)S(1)}, u32[]{:S(2)}, u32[]{:S(2)}) %collective-permute-start.10) | collective-permute-done | bytes 524320 | tf_op jit(solution)/shard_map/ppermute | solution.py:21
  459.9 7.8 %collective-permute-done.11 = bf16[128,2048]{0,1:T(8,128)(2,1)S(1)} collective-permute-done((bf16[128,2048]{0,1:T(8,128)(2,1)S(1)}, bf16[128,2048]{0,1:T(8,128)(2,1)S(1)}, u32[]{:S(2)}, u32[]{:S(2)}) %collective-permute-start.11) | collective-permute-done | bytes 524320 | tf_op jit(solution)/shard_map/ppermute | solution.py:21
  467.7 11.2 %collective-permute-done.12 = bf16[128,2048]{0,1:T(8,128)(2,1)S(1)} collective-permute-done((bf16[128,2048]{0,1:T(8,128)(2,1)S(1)}, bf16[128,2048]{0,1:T(8,128)(2,1)S(1)}, u32[]{:S(2)}, u32[]{:S(2)}) %collective-permute-start.12) | collective-permute-done | bytes 524320 | tf_op jit(solution)/shard_map/ppermute | solution.py:21
  479.0 11.8 %collective-permute-done.13 = bf16[128,2048]{0,1:T(8,128)(2,1)S(1)} collective-permute-done((bf16[128,2048]{0,1:T(8,128)(2,1)S(1)}, bf16[128,2048]{0,1:T(8,128)(2,1)S(1)}, u32[]{:S(2)}, u32[]{:S(2)}) %collective-permute-start.13) | collective-permute-done | bytes 524320 | tf_op jit(solution)/shard_map/ppermute | solution.py:21
  492.5 6.5 fusion.22
  499.0 12.7 %copy.97 = bf16[2304,2048]{1,0:T(8,128)(2,1)} copy(bf16[2304,2048]{0,1:T(8,128)(2,1)} %fusion.22) | data formatting | bytes 18874368
  511.8 144.0 %reduce-scatter.7.cloned.1.call-done = bf16[144,2048]{1,0:T(8,128)(2,1)} async-done(((bf16[2304,2048]{1,0:T(8,128)(2,1)}), bf16[144,2048]{1,0:T(8,128)(2,1)}) %reduce-scatter.7.cloned.1.call-update) | async-done | bytes 589840
  655.8 2.2 copy.98
  658.0 7.8 %fusion.23 = bf16[1,128,2304]{2,1,0:T(8,128)(2,1)} fusion(bf16[2304,2048]{1,0:T(8,128)(2,1)} %all-gather.2.cloned.1.call-done, bf16[128,1024]{0,1:T(8,128)(2,1)S(1)} %slice.169, bf16[128,1024]{0,1:T(8,128)(2,1)S(1)} %bitcast.165), kind=kOutput, calls=%fused_computation.55 | convolution fusion | flops 1209303040 | bytes 10551296 | tf_op jit(solution)/shard_map/dot_general | solution.py:163
  665.8 42.9 %reduce-scatter.5.cloned.1.call-done = bf16[144,128]{0,1:T(8,128)(2,1)} async-done(((bf16[144,2048]{0,1:T(8,128)(2,1)}), bf16[144,128]{0,1:T(8,128)(2,1)}) %reduce-scatter.5.cloned.1.call-update) | async-done | bytes 36880 | tf_op jit(solution)/shard_map/reduce_scatter | solution.py:174
  (153 shorter events, 70.6 us)
Async XLA Ops:
  7.2 84.9 %copy-start = (bf16[1,128,2304]{2,1,0:T(8,128)(2,1)S(1)}, bf16[1,128,2304]{2,1,0:T(8,128)(2,1)}, u32[]{:S(2)}) copy-start(bf16[1,128,2304]{2,1,0:T(8,128)(2,1)} %param.7) | copy-start | bytes 1769476
  7.2 84.9 %all-gather.2.cloned.1.call-start = ((), (), s32[]{:S(2)}) async-start(), calls=%async_computation.2 | async-start | bytes 10027008 | tf_op jit(solution)/shard_map/all_gather | solution.py:125
  7.9 647.9 %reduce-scatter.7.cloned.1.call-start = ((), (), s32[]{:S(2)}) async-start(), calls=%async_computation.4 | async-start | bytes 10027008
  11.6 85.7 %copy-start.6 = (f32[128,64]{1,0:T(8,128)}, f32[128,64]{1,0:T(8,128)S(1)}, u32[]{:S(2)}) copy-start(f32[128,64]{1,0:T(8,128)S(1)} %get-tuple-element.364) | copy-start | bytes 98308
  97.1 5.3 copy-start.8
  97.1 5.6 copy-start.9
  97.9 77.1 %collective-permute-start = (bf16[128,2048]{1,0:T(8,128)(2,1)S(1)}, bf16[128,2048]{1,0:T(8,128)(2,1)}, u32[]{:S(2)}, u32[]{:S(2)}) collective-permute-start(bf16[128,2048]{1,0:T(8,128)(2,1)S(1)} %pad_maximum_fusion.1), channel_id=1, source_target_pairs={{0,128},{16,144},{32,160},{48,176},{64,192},{80,208},{96,224},{112... | collective-permute-start | bytes 1572872 | tf_op jit(solution)/shard_map/ppermute | solution.py:21
  99.2 84.8 %collective-permute-start.1 = (bf16[128,2048]{1,0:T(8,128)(2,1)S(1)}, bf16[128,2048]{1,0:T(8,128)(2,1)}, u32[]{:S(2)}, u32[]{:S(2)}) collective-permute-start(bf16[128,2048]{1,0:T(8,128)(2,1)S(1)} %pad_maximum_fusion.1), channel_id=1, source_target_pairs={{0,112},{16,128},{32,144},{48,160},{64,176},{80,192},{96,208},{112... | collective-permute-start | bytes 1572872 | tf_op jit(solution)/shard_map/ppermute | solution.py:21
  100.6 86.6 %collective-permute-start.2 = (bf16[128,2048]{1,0:T(8,128)(2,1)S(1)}, bf16[128,2048]{1,0:T(8,128)(2,1)}, u32[]{:S(2)}, u32[]{:S(2)}) collective-permute-start(bf16[128,2048]{1,0:T(8,128)(2,1)S(1)} %pad_maximum_fusion.1), channel_id=1, source_target_pairs={{0,96},{16,112},{32,128},{48,144},{64,160},{80,176},{96,192},{112,... | collective-permute-start | bytes 1572872 | tf_op jit(solution)/shard_map/ppermute | solution.py:21
  103.8 142.1 %collective-permute-start.7 = (bf16[128,2048]{1,0:T(8,128)(2,1)S(1)}, bf16[128,2048]{1,0:T(8,128)(2,1)S(1)}, u32[]{:S(2)}, u32[]{:S(2)}) collective-permute-start(bf16[128,2048]{1,0:T(8,128)(2,1)S(1)} %pad_maximum_fusion.1), channel_id=1, source_target_pairs={{0,16},{16,32},{32,48},{48,64},{64,80},{80,96},{96,112},{112,128},... | collective-permute-start | bytes 1572872 | tf_op jit(solution)/shard_map/ppermute | solution.py:21
  105.7 139.4 %collective-permute-start.6 = (bf16[128,2048]{1,0:T(8,128)(2,1)S(1)}, bf16[128,2048]{1,0:T(8,128)(2,1)S(1)}, u32[]{:S(2)}, u32[]{:S(2)}) collective-permute-start(bf16[128,2048]{1,0:T(8,128)(2,1)S(1)} %pad_maximum_fusion.1), channel_id=1, source_target_pairs={{0,32},{16,48},{32,64},{48,80},{64,96},{80,112},{96,128},{112,144}... | collective-permute-start | bytes 1572872 | tf_op jit(solution)/shard_map/ppermute | solution.py:21
  175.0 49.4 %collective-permute-start.3 = (bf16[128,2048]{1,0:T(8,128)(2,1)S(1)}, bf16[128,2048]{1,0:T(8,128)(2,1)S(1)}, u32[]{:S(2)}, u32[]{:S(2)}) collective-permute-start(bf16[128,2048]{1,0:T(8,128)(2,1)S(1)} %pad_maximum_fusion.1), channel_id=1, source_target_pairs={{0,80},{16,96},{32,112},{48,128},{64,144},{80,160},{96,176},{112,1... | collective-permute-start | bytes 1572872 | tf_op jit(solution)/shard_map/ppermute | solution.py:21
  184.0 59.4 %collective-permute-start.4 = (bf16[128,2048]{1,0:T(8,128)(2,1)S(1)}, bf16[128,2048]{1,0:T(8,128)(2,1)S(1)}, u32[]{:S(2)}, u32[]{:S(2)}) collective-permute-start(bf16[128,2048]{1,0:T(8,128)(2,1)S(1)} %pad_maximum_fusion.1), channel_id=1, source_target_pairs={{0,64},{16,80},{32,96},{48,112},{64,128},{80,144},{96,160},{112,17... | collective-permute-start | bytes 1572872 | tf_op jit(solution)/shard_map/ppermute | solution.py:21
  187.2 57.0 %collective-permute-start.5 = (bf16[128,2048]{1,0:T(8,128)(2,1)S(1)}, bf16[128,2048]{1,0:T(8,128)(2,1)S(1)}, u32[]{:S(2)}, u32[]{:S(2)}) collective-permute-start(bf16[128,2048]{1,0:T(8,128)(2,1)S(1)} %pad_maximum_fusion.1), channel_id=1, source_target_pairs={{0,48},{16,64},{32,80},{48,96},{64,112},{80,128},{96,144},{112,160... | collective-permute-start | bytes 1572872 | tf_op jit(solution)/shard_map/ppermute | solution.py:21
  260.0 5.0 copy-start.3
  262.8 4.3 copy-start.2
  265.1 1.5 copy-start.1
  265.1 1.5 copy-start.11
  273.5 4.8 copy-start.5
  278.3 0.8 copy-start.4
  278.3 5.1 copy-start.3
  281.0 4.3 copy-start.2
  283.3 1.5 copy-start.1
  283.3 1.5 copy-start.11
  291.7 4.7 copy-start.5
  296.5 0.8 copy-start.4
  296.5 5.0 copy-start.3
  299.2 4.3 copy-start.2
  301.5 1.5 copy-start.1
  301.5 1.5 copy-start.11
  310.0 4.8 copy-start.5
  314.7 0.8 copy-start.4
  314.8 5.0 copy-start.3
  317.5 4.3 copy-start.2
  319.8 1.5 copy-start.1
  319.8 1.5 copy-start.11
  328.2 4.8 copy-start.5
  340.8 40.5 %collective-permute-start.8 = (bf16[128,2048]{0,1:T(8,128)(2,1)S(1)}, bf16[128,2048]{0,1:T(8,128)(2,1)S(1)}, u32[]{:S(2)}, u32[]{:S(2)}) collective-permute-start(bf16[128,2048]{0,1:T(8,128)(2,1)S(1)} %get-tuple-element.348), channel_id=1, source_target_pairs={{16,0},{32,16},{48,32},{64,48},{80,64},{96,80},{112,96},{128,112},... | collective-permute-start | bytes 1572872 | tf_op jit(solution)/shard_map/ppermute | solution.py:21
  352.5 92.7 %collective-permute-start.9 = (bf16[128,2048]{0,1:T(8,128)(2,1)S(1)}, bf16[128,2048]{0,1:T(8,128)(2,1)S(1)}, u32[]{:S(2)}, u32[]{:S(2)}) collective-permute-start(bf16[128,2048]{0,1:T(8,128)(2,1)S(1)} %get-tuple-element.349), channel_id=1, source_target_pairs={{32,0},{48,16},{64,32},{80,48},{96,64},{112,80},{128,96},{144,112}... | collective-permute-start | bytes 1572872 | tf_op jit(solution)/shard_map/ppermute | solution.py:21
  371.2 85.3 %collective-permute-start.10 = (bf16[128,2048]{0,1:T(8,128)(2,1)S(1)}, bf16[128,2048]{0,1:T(8,128)(2,1)S(1)}, u32[]{:S(2)}, u32[]{:S(2)}) collective-permute-start(bf16[128,2048]{0,1:T(8,128)(2,1)S(1)} %get-tuple-element.350), channel_id=1, source_target_pairs={{48,0},{64,16},{80,32},{96,48},{112,64},{128,80},{144,96},{160,112... | collective-permute-start | bytes 1572872 | tf_op jit(solution)/shard_map/ppermute | solution.py:21
  378.0 89.7 %collective-permute-start.11 = (bf16[128,2048]{0,1:T(8,128)(2,1)S(1)}, bf16[128,2048]{0,1:T(8,128)(2,1)S(1)}, u32[]{:S(2)}, u32[]{:S(2)}) collective-permute-start(bf16[128,2048]{0,1:T(8,128)(2,1)S(1)} %get-tuple-element.351), channel_id=1, source_target_pairs={{64,0},{80,16},{96,32},{112,48},{128,64},{144,80},{160,96},{176,11... | collective-permute-start | bytes 1572872 | tf_op jit(solution)/shard_map/ppermute | solution.py:21
  379.9 99.1 %collective-permute-start.12 = (bf16[128,2048]{0,1:T(8,128)(2,1)S(1)}, bf16[128,2048]{0,1:T(8,128)(2,1)S(1)}, u32[]{:S(2)}, u32[]{:S(2)}) collective-permute-start(bf16[128,2048]{0,1:T(8,128)(2,1)S(1)} %get-tuple-element.352), channel_id=1, source_target_pairs={{80,0},{96,16},{112,32},{128,48},{144,64},{160,80},{176,96},{192,1... | collective-permute-start | bytes 1572872 | tf_op jit(solution)/shard_map/ppermute | solution.py:21
  381.2 109.5 %collective-permute-start.13 = (bf16[128,2048]{0,1:T(8,128)(2,1)S(1)}, bf16[128,2048]{0,1:T(8,128)(2,1)S(1)}, u32[]{:S(2)}, u32[]{:S(2)}) collective-permute-start(bf16[128,2048]{0,1:T(8,128)(2,1)S(1)} %get-tuple-element.353), channel_id=1, source_target_pairs={{96,0},{112,16},{128,32},{144,48},{160,64},{176,80},{192,96},{208,... | collective-permute-start | bytes 1572872 | tf_op jit(solution)/shard_map/ppermute | solution.py:21
  445.2 45.5 %collective-permute-start.15 = (bf16[128,2048]{0,1:T(8,128)(2,1)S(1)}, bf16[128,2048]{0,1:T(8,128)(2,1)S(1)}, u32[]{:S(2)}, u32[]{:S(2)}) collective-permute-start(bf16[128,2048]{0,1:T(8,128)(2,1)S(1)} %get-tuple-element.354), channel_id=1, source_target_pairs={{128,0},{144,16},{160,32},{176,48},{192,64},{208,80},{224,96},{240... | collective-permute-start | bytes 1572872 | tf_op jit(solution)/shard_map/ppermute | solution.py:21
  456.4 34.3 %collective-permute-start.14 = (bf16[128,2048]{0,1:T(8,128)(2,1)S(1)}, bf16[128,2048]{0,1:T(8,128)(2,1)S(1)}, u32[]{:S(2)}, u32[]{:S(2)}) collective-permute-start(bf16[128,2048]{0,1:T(8,128)(2,1)S(1)} %get-tuple-element.355), channel_id=1, source_target_pairs={{112,0},{128,16},{144,32},{160,48},{176,64},{192,80},{208,96},{224... | collective-permute-start | bytes 1572872 | tf_op jit(solution)/shard_map/ppermute | solution.py:21
  459.9 32.0 %copy-start.7 = (f32[128,64]{1,0:T(8,128)S(1)}, f32[128,64]{1,0:T(8,128)}, u32[]{:S(2)}) copy-start(f32[128,64]{1,0:T(8,128)} %copy-done.6) | copy-start | bytes 98308
  459.9 32.0 %copy-start.10 = (f32[128,64]{1,0:T(8,128)S(1)}, f32[128,64]{1,0:T(8,128)}, u32[]{:S(2)}) copy-start(f32[128,64]{1,0:T(8,128)} %get-tuple-element.362) | copy-start | bytes 98308
  511.7 197.0 %reduce-scatter.5.cloned.1.call-start = ((), (), s32[]{:S(2)}) async-start(), calls=%async_computation.3 | async-start | bytes 1114112 | tf_op jit(solution)/shard_map/reduce_scatter | solution.py:174
  (1 other events, 0.8 us)
Sparse Core Ops, SparseCore 0:
  10.5 81.5 all-gather.1
  511.8 143.9 reduce-scatter.6
  658.5 50.2 reduce-scatter.4
where the time goes:
time: 727 us; the launch traced here: 717 us
  waiting for transfers between devices  492 us (68%)
  local copies, waits for them, and re-layouts  79.2 us (11%)
  starting transfers between devices  60.7 us (8%)
  matrix products  42.6 us (6%)
  other arithmetic  27.7 us (4%)
  between operations  14.2 us (2%)
    ppermute x16, waiting for transfers between devices, from_behind(): lax.ppermute(value, axis, [(source, source + steps) for source in range(f...  224 us
    unnamed x4, waiting for transfers between devices  145 us
    all_gather x1, waiting for transfers between devices, on_device(): weight_full = lax.all_gather(w_kv, 'fsdp', axis=0, tiled=True)  80.4 us
    ppermute x16, starting transfers between devices, from_behind(): lax.ppermute(value, axis, [(source, source + steps) for source in range(f...  60.6 us
    reduce_scatter x1, waiting for transfers between devices, on_device(): lax.psum_scatter(shared, 'seq', scatter_dimension=1, tiled=True)  42.9 us
    unnamed x31, local copies, waits for them, and re-layouts  35 us
  transfers between devices with their start and end apart: 19, of which 12 were waited for; matrix products, arithmetic and copies ran while one was open for 3% of the time, Pallas kernels for 0%

commit v1 on v0

v1 whole, which is shorter than its diff:
```python
import functools

import jax
import jax.numpy as jnp
from jax import lax
from jax.experimental import pallas as pl
from jax.experimental.pallas import tpu as pltpu
from jax.sharding import PartitionSpec as P

D = 2304
HD = 128
WIN = 1024
SEQLEN = 2048
NDOC = 8
NZ = 8
NX = 4
NY = 4
ROWS = D // (NX * NY)
HALF = 1024
PART = 512
TOK = 128
CTOK = 256
CAP = 50.0
SCALE = 1.0 / 12.0
ROPE_BASE = 10000.0
MESH = pl.DeviceIdType.MESH
ANY = pl.BlockSpec(memory_space=pl.ANY)
VM = pl.BlockSpec(memory_space=pltpu.VMEM)
BF = jnp.bfloat16
F32 = jnp.float32


def where_am_i():
    s = lax.axis_index("seq")
    f = lax.axis_index("fsdp")
    z = s // 2
    c = s - 2 * z
    x = f // NY
    y = f - NY * x
    return s, f, z, c, x, y


def ring(v, n):
    return lax.rem(v + n, n)


def remote(src, dst, send, recv, s, f):
    return pltpu.make_async_remote_copy(
        src_ref=src,
        dst_ref=dst,
        send_sem=send,
        recv_sem=recv,
        device_id={"seq": s, "fsdp": f},
        device_id_type=MESH,
    )


def enter(s, f, x, y):
    barrier = pltpu.get_barrier_semaphore()
    for step in range(1, 2 * NZ):
        pl.semaphore_signal(
            barrier,
            inc=1,
            device_id={"seq": ring(s + step, 2 * NZ), "fsdp": f},
            device_id_type=MESH,
        )
    for dx, dy in ((1, 0), (-1, 0), (0, 1), (0, -1)):
        pl.semaphore_signal(
            barrier,
            inc=1,
            device_id={"seq": s, "fsdp": ring(x + dx, NX) * NY + ring(y + dy, NY)},
            device_id_type=MESH,
        )
    pl.semaphore_wait(barrier, 2 * NZ - 1 + 4)


def rotated(values, cosine, sine):
    return values * cosine + pltpu.roll(values, HD // 2, 1) * sine


def k1_kernel(
    x_ref,
    q_ref,
    w_ref,
    g_ref,
    cos_ref,
    sin_ref,
    qh_ref,
    gh_ref,
    kv_ref,
    xt_ref,
    wh_ref,
    wg,
    xs,
    proj,
    wl_sem,
    xl_sem,
    xr_sem,
    ws_sem,
    wr_sem,
    ql_sem,
    qs_sem,
    qr_sem,
    ks_sem,
    kr_sem,
    fs_sem,
    fr_sem,
    o_sem,
):
    s, f, z, c, x, y = where_am_i()
    sib = s + 1 - 2 * c
    own_rows = pl.ds(pl.multiple_of(f * ROWS, 16), ROWS)
    load_w = []
    for k in range(8):
        cols = pl.ds(pl.multiple_of((2 * k + c) * HD, HD), HD)
        load_w.append(
            pltpu.make_async_copy(
                w_ref.at[:, cols], wg.at[own_rows, pl.ds(k * HD, HD)], wl_sem.at[k]
            )
        )
    for copy in load_w:
        copy.start()
    own_tok = pl.ds(pl.multiple_of(c * TOK, TOK), TOK)
    load_x = pltpu.make_async_copy(x_ref, xs.at[own_tok], xl_sem)
    load_x.start()
    enter(s, f, x, y)

    def piece(part, off, half=None):
        origin = ring(x + off[0], NX) * NY + ring(y + off[1], NY)
        rows = pl.ds(pl.multiple_of(origin * ROWS, 16), ROWS)
        if half is None:
            return wg.at[rows, pl.ds(part * PART, PART)]
        return wg.at[rows, pl.ds(part * PART + half * (PART // 2), PART // 2)]

    sends = []

    def pass_on(part, off, step, half=None):
        there = tuple((o - d) % 4 for o, d in zip(off, step))
        there = tuple(-1 if t == 3 else t for t in there)
        ref = piece(part, off, half)
        copy = remote(
            ref,
            ref,
            ws_sem.at[len(sends)],
            wr_sem.at[part, there[0] + 1, there[1] + 1, half or 0],
            s,
            ring(x + step[0], NX) * NY + ring(y + step[1], NY),
        )
        copy.start()
        sends.append(copy)

    def arrived(part, off, half=None):
        ref = piece(part, off, half)
        remote(
            ref, ref, ws_sem.at[0], wr_sem.at[part, off[0] + 1, off[1] + 1, half or 0], s, f
        ).wait_recv()

    def at(part, a, b):
        return (a, b) if part == 0 else (b, a)

    for copy in load_w:
        copy.wait()
    for part in range(2):
        for d in (1, -1):
            pass_on(part, (0, 0), at(part, d, 0))
    for part in range(2):
        for d in (1, -1):
            pass_on(part, (0, 0), at(part, 0, d))
    load_x.wait()
    give_x = remote(xs.at[own_tok], xs.at[own_tok], xr_sem.at[0], xr_sem.at[1], sib, f)
    give_x.start()

    own_seq = pl.ds(pl.multiple_of(s * TOK, TOK), TOK)
    own_head = pl.ds(pl.multiple_of(s * HD, HD), HD)
    keep = []
    for i, (src, dst) in enumerate(((q_ref, qh_ref), (g_ref, gh_ref))):
        keep.append(pltpu.make_async_copy(src.at[:, own_head], dst.at[own_seq], ql_sem.at[i]))
        keep[-1].start()
    for step in range(1, 2 * NZ):
        to = ring(s + step, 2 * NZ)
        head = pl.ds(pl.multiple_of(to * HD, HD), HD)
        for i, (src, dst) in enumerate(((q_ref, qh_ref), (g_ref, gh_ref))):
            remote(src.at[:, head], dst.at[own_seq], qs_sem.at[i], qr_sem.at[i], to, f).start()

    for d in (-1, 1):
        for part in range(2):
            arrived(part, at(part, d, 0))
            pass_on(part, at(part, d, 0), at(part, -d, 0), 0 if d < 0 else 1)
            for e in (1, -1):
                pass_on(part, at(part, d, 0), at(part, 0, e))
    for d in (-1, 1):
        for part in range(2):
            arrived(part, at(part, 0, d))
            pass_on(part, at(part, 0, d), at(part, 0, -d), 0 if d < 0 else 1)
    for part in range(2):
        arrived(part, at(part, 2, 0), 0)
        arrived(part, at(part, 2, 0), 1)
        for e in (1, -1):
            pass_on(part, at(part, 2, 0), at(part, 0, e))
    remote(xs.at[own_tok], xs.at[own_tok], xr_sem.at[0], xr_sem.at[1], sib, f).wait_recv()

    def turn(i, carry):
        cols = pl.ds(pl.multiple_of(i * 256, 256), 256)
        xt_ref[cols, :] = xs[:, cols].T
        return carry

    lax.fori_loop(0, D // 256, turn, 0)
    for a in (-1, 1, 2):
        for d in (-1, 1):
            for part in range(2):
                arrived(part, at(part, a, d))
                pass_on(part, at(part, a, d), at(part, 0, -d), 0 if d < 0 else 1)
    for a in (0, -1, 1, 2):
        for part in range(2):
            arrived(part, at(part, a, 2), 0)
            arrived(part, at(part, a, 2), 1)
    save_w = pltpu.make_async_copy(wg, wh_ref, o_sem)
    save_w.start()

    def kv_copy(k):
        kind = k // 4
        head = 2 * (k % 4) + c
        to = 2 * head + kind
        rows = pl.ds(pl.multiple_of(z * CTOK, CTOK), CTOK)
        local = pltpu.make_async_copy(proj.at[k], kv_ref.at[kind, rows], kr_sem)
        away = remote(proj.at[k], kv_ref.at[kind, rows], ks_sem.at[k], kr_sem, to, f)
        return to == s, local, away

    for t in range(4):
        res = jnp.dot(xs[...], wg[:, t * 256 : (t + 1) * 256], preferred_element_type=F32)
        for j in range(2):
            k = 2 * t + j
            block = res[:, j * HD : (j + 1) * HD]
            if k < 4:
                block = rotated(block, cos_ref[...], sin_ref[...])
            proj[k] = block.astype(BF)
            mine, local, away = kv_copy(k)

            @pl.when(mine)
            def _():
                local.start()

            @pl.when(jnp.logical_not(mine))
            def _():
                away.start()

    for copy in sends:
        copy.wait_send()
    give_x.wait_send()
    for copy in keep:
        copy.wait()
    for i, (src, dst) in enumerate(((q_ref, qh_ref), (g_ref, gh_ref))):
        others = dst.at[pl.ds(0, SEQLEN - TOK)]
        whole = remote(others, others, qs_sem.at[i], qr_sem.at[i], sib, f)
        whole.wait_send()
        whole.wait_recv()
    got = kv_ref.at[c]
    pltpu.make_async_copy(got, got, kr_sem).wait()
    share = remote(got, got, fs_sem, fr_sem, sib, f)
    share.start()
    for k in range(8):
        mine, local, away = kv_copy(k)

        @pl.when(jnp.logical_not(mine))
        def _():
            away.wait_send()

    share.wait()
    save_w.wait()


def k1(x, q, w, g, cosine, sine):
    dma = pltpu.SemaphoreType.DMA
    seq_block = jax.ShapeDtypeStruct((SEQLEN, HD), BF)
    return pl.pallas_call(
        k1_kernel,
        out_shape=(
            seq_block,
            seq_block,
            jax.ShapeDtypeStruct((2, SEQLEN, HD), BF),
            jax.ShapeDtypeStruct((D, CTOK), BF),
            jax.ShapeDtypeStruct((D, HALF), BF),
        ),
        in_specs=[ANY, ANY, ANY, ANY, VM, VM],
        out_specs=(ANY, ANY, ANY, VM, ANY),
        scratch_shapes=[
            pltpu.VMEM((D, HALF), BF),
            pltpu.VMEM((CTOK, D), BF),
            pltpu.VMEM((8, CTOK, HD), BF),
            dma((8,)),
            dma(()),
            dma((2,)),
            dma((40,)),
            dma((2, 4, 4, 2)),
            dma((2,)),
            dma((2,)),
            dma((2,)),
            dma((8,)),
            dma(()),
            dma(()),
            dma(()),
            dma(()),
        ],
        compiler_params=pltpu.CompilerParams(
            collective_id=0, has_side_effects=True, vmem_limit_bytes=40 << 20
        ),
        name="gather_project",
    )(x, q, w, g, cosine, sine)


QT = 256
KT = 256
NT = (((1,), (1,)), ((), ()))


def k2_kernel(len_ref, q_ref, g_ref, kv_ref, o_ref, dkv_ref, vt, wbuf, tbuf, dk, dv):
    ends = []
    total = 0
    for i in range(NDOC):
        total = total + len_ref[i]
        ends.append(total)
    dk[...] = jnp.zeros_like(dk)
    dv[...] = jnp.zeros_like(dv)

    def flip(i, carry):
        rows = pl.ds(pl.multiple_of(i * KT, KT), KT)
        vt[:, rows] = kv_ref[1, rows, :].T
        return carry

    lax.fori_loop(0, SEQLEN // KT, flip, 0)

    def one_tile(i, carry):
        base = i * QT
        rows = pl.ds(pl.multiple_of(base, QT), QT)
        qt = q_ref[rows, :]
        gt = g_ref[rows, :]
        pos = base + lax.broadcasted_iota(jnp.int32, (1, QT), 1)
        start = jnp.zeros((1, QT), jnp.int32)
        first = jnp.int32(0)
        for end in ends:
            start = jnp.where(pos >= end, end, start)
            first = jnp.where(base >= end, end, first)
        low = jnp.maximum(start, pos - (WIN - 1))
        first = jnp.maximum(first, base - (WIN - 1)) // KT

        def forward(t, state):
            acc, norm = state
            krows = pl.ds(pl.multiple_of(t * KT, KT), KT)
            st = lax.dot_general(kv_ref[0, krows, :], qt, NT, preferred_element_type=F32)
            squashed = jnp.tanh(st * (SCALE / CAP))
            key = t * KT + lax.broadcasted_iota(jnp.int32, (KT, QT), 0)
            allowed = (key <= pos) & (key >= low)
            weight = jnp.where(allowed, jnp.exp(CAP * squashed), 0.0)
            slot = t - first
            wbuf[slot] = weight
            tbuf[slot] = squashed
            norm = norm + jnp.sum(weight, axis=0, keepdims=True)
            acc = acc + jnp.dot(vt[:, krows], weight.astype(BF), preferred_element_type=F32)
            return acc, norm

        acc, norm = lax.fori_loop(
            first, i + 1, forward, (jnp.zeros((HD, QT), F32), jnp.zeros((1, QT), F32))
        )
        inverse = 1.0 / norm
        out_t = (acc * inverse).astype(BF)
        out = out_t.astype(F32).T
        o_ref[rows, :] = out.astype(BF)
        delta = jnp.sum(gt.astype(F32).T * out_t.astype(F32), axis=0, keepdims=True)

        def backward(t, carry2):
            krows = pl.ds(pl.multiple_of(t * KT, KT), KT)
            slot = t - first
            probs = wbuf[slot] * inverse
            squashed = tbuf[slot]
            dprob = lax.dot_general(kv_ref[1, krows, :], gt, NT, preferred_element_type=F32)
            dscore = probs * (dprob - delta) * (1.0 - squashed * squashed)
            dk[krows, :] += jnp.dot(dscore.astype(BF), qt, preferred_element_type=F32)
            dv[krows, :] += jnp.dot(probs.astype(BF), gt, preferred_element_type=F32)
            return carry2

        lax.fori_loop(first, i + 1, backward, 0)
        return carry

    lax.fori_loop(0, SEQLEN // QT, one_tile, 0)
    dkv_ref[0] = (dk[...] * SCALE).astype(BF)
    dkv_ref[1] = dv[...].astype(BF)


def k2(lengths, qh, gh, kv):
    return pl.pallas_call(
        k2_kernel,
        out_shape=(
            jax.ShapeDtypeStruct((SEQLEN, HD), BF),
            jax.ShapeDtypeStruct((2, SEQLEN, HD), BF),
        ),
        in_specs=[pl.BlockSpec(memory_space=pltpu.SMEM), VM, VM, VM],
        out_specs=(VM, VM),
        scratch_shapes=[
            pltpu.VMEM((HD, SEQLEN), BF),
            pltpu.VMEM((5, KT, QT), F32),
            pltpu.VMEM((5, KT, QT), F32),
            pltpu.VMEM((SEQLEN, HD), F32),
            pltpu.VMEM((SEQLEN, HD), F32),
        ],
        compiler_params=pltpu.CompilerParams(vmem_limit_bytes=40 << 20),
        name="attend",
    )(lengths, qh, gh, kv)


def k3_kernel(
    o_ref,
    dkv_ref,
    xt_ref,
    wh_ref,
    cos_ref,
    sin_ref,
    out_ref,
    gin_ref,
    gw_ref,
    wv,
    mine,
    theirs,
    total,
    got,
    dd,
    gi,
    gsend,
    grecv,
    part_sum,
    r1,
    r2,
    second,
    r3,
    r4,
    third,
    zr,
    l_sem,
    sib_sem,
    ds_sem,
    dr_sem,
    ol_sem,
    os_sem,
    or_sem,
    g_sem,
    s1_sem,
    r1_sem,
    s2_sem,
    r2_sem,
    s3_sem,
    r3_sem,
    s4_sem,
    r4_sem,
    zs_sem,
    zr_sem,
):
    s, f, z, c, x, y = where_am_i()
    sib = s + 1 - 2 * c
    load_w = pltpu.make_async_copy(wh_ref, wv, l_sem.at[0])
    load_d = pltpu.make_async_copy(dkv_ref.at[c], mine, l_sem.at[1])
    load_d.start()
    load_w.start()
    enter(s, f, x, y)
    swap = remote(dkv_ref.at[1 - c], theirs, sib_sem.at[0], sib_sem.at[1], sib, f)
    swap.start()
    load_d.wait()
    swap.wait_recv()
    slot = 4 * c + z // 2
    target = 2 * ring(z, NZ) + lax.rem(z, 2)

    def d_copy(step):
        chip = ring(z + step, NZ)
        rows = pl.ds(pl.multiple_of(chip * CTOK, CTOK), CTOK)
        to = 2 * chip + lax.rem(z, 2)
        return rows, remote(total.at[rows], got.at[slot], ds_sem.at[step], dr_sem, to, f)

    for step in (4, 3, 5, 2, 6, 1, 7):
        rows, copy = d_copy(step)
        total[rows, :] = (mine[rows, :].astype(F32) + theirs[rows, :].astype(F32)).astype(BF)
        copy.start()
    rows, copy = d_copy(0)
    total[rows, :] = (mine[rows, :].astype(F32) + theirs[rows, :].astype(F32)).astype(BF)
    local = pltpu.make_async_copy(total.at[rows], got.at[slot], dr_sem)

    @pl.when(target == s)
    def _():
        local.start()

    @pl.when(target != s)
    def _():
        copy.start()

    own_head = pl.ds(pl.multiple_of(s * HD, HD), HD)
    own_seq = pl.ds(pl.multiple_of(s * TOK, TOK), TOK)
    keep_o = pltpu.make_async_copy(o_ref.at[own_seq], out_ref.at[:, own_head], ol_sem)
    keep_o.start()
    for step in range(1, 2 * NZ):
        to = ring(s + step, 2 * NZ)
        theirs_tok = pl.ds(pl.multiple_of(to * TOK, TOK), TOK)
        remote(
            o_ref.at[theirs_tok], out_ref.at[:, own_head], os_sem, or_sem, to, f
        ).start()

    pltpu.make_async_copy(got, got, dr_sem).wait()
    for k in range(8):
        block = got[k]
        if k < 4:
            block = rotated(block.astype(F32), cos_ref[...], -sin_ref[...]).astype(BF)
        dd[:, k * HD : (k + 1) * HD] = block

    def term(part, cx, cy):
        rows = pl.ds(pl.multiple_of((cx * NY + cy) * ROWS, 16), ROWS)
        cols = pl.ds(part * PART, PART)
        part_sum[part, cx, cy] = jnp.dot(
            xt_ref[rows, :], dd[:, cols], preferred_element_type=F32
        ).astype(BF)

    def chunk(part, a):
        for j in range(4):
            if part == 0:
                term(part, a, j)
            else:
                term(part, j, a)

    def chunk_ref(part, a, cols):
        if part == 0:
            return part_sum.at[part, a, :, :, cols]
        return part_sum.at[part, :, a, :, cols]

    first_axis = (x, y)
    second_axis = (y, x)

    def neighbour(part, level, d):
        along_x = (part == 0) == (level == 0)
        if along_x:
            return ring(x + d, NX) * NY + y
        return x * NY + ring(y + d, NY)

    halves = (pl.ds(0, PART // 2), pl.ds(PART // 2, PART // 2))
    full = pl.ds(0, PART)
    dirs = (1, -1)
    sent = []
    for part in range(2):
        far = ring(first_axis[part] + 2, 4)
        chunk(part, far)
        for h, d in enumerate(dirs):
            copy = remote(
                chunk_ref(part, far, halves[h]),
                r1.at[part, h],
                s1_sem.at[part, h],
                r1_sem.at[part, h],
                s,
                neighbour(part, 0, d),
            )
            copy.start()
            sent.append(copy)
    for part in range(2):
        for d in (1, -1, 0):
            chunk(part, ring(first_axis[part] + d, 4))
    for part in range(2):
        for h, d in enumerate(dirs):
            near = ring(first_axis[part] + d, 4)
            remote(
                r1.at[part, h], r1.at[part, h], s1_sem.at[part, h], r1_sem.at[part, h], s, f
            ).wait_recv()
            cols = slice(h * (PART // 2), (h + 1) * (PART // 2))
            for j in range(4):
                idx = (part, near, j) if part == 0 else (part, j, near)
                part_sum[idx + (slice(None), cols)] = (
                    part_sum[idx + (slice(None), cols)].astype(F32)
                    + r1[part, h, j].astype(F32)
                ).astype(BF)
            copy = remote(
                chunk_ref(part, near, full),
                r2.at[part, h],
                s2_sem.at[part, h],
                r2_sem.at[part, h],
                s,
                neighbour(part, 0, d),
            )
            copy.start()
            sent.append(copy)

    load_w.wait()

    def input_tile(i, carry):
        rows = pl.ds(pl.multiple_of(i * 256, 256), 256)
        gi[:, rows] = lax.dot_general(dd[...], wv[rows, :], NT, preferred_element_type=F32)
        return carry

    lax.fori_loop(0, D // 256, input_tile, 0)
    other_tok = pl.ds(pl.multiple_of((1 - c) * TOK, TOK), TOK)
    own_tok = pl.ds(pl.multiple_of(c * TOK, TOK), TOK)
    gsend[...] = gi[other_tok, :].astype(BF)
    give = remote(gsend, grecv, g_sem.at[0], g_sem.at[1], sib, f)
    give.start()

    for part in range(2):
        for h in range(2):
            remote(
                r2.at[part, h], r2.at[part, h], s2_sem.at[part, h], r2_sem.at[part, h], s, f
            ).wait_recv()
        for j in range(4):
            idx = (part, x, j) if part == 0 else (part, j, y)
            second[part, j] = (
                part_sum[idx].astype(F32)
                + r2[part, 0, j].astype(F32)
                + r2[part, 1, j].astype(F32)
            ).astype(BF)
        far = ring(second_axis[part] + 2, 4)
        for h, d in enumerate(dirs):
            copy = remote(
                second.at[part, far, :, halves[h]],
                r3.at[part, h],
                s3_sem.at[part, h],
                r3_sem.at[part, h],
                s,
                neighbour(part, 1, d),
            )
            copy.start()
            sent.append(copy)
    for part in range(2):
        for h, d in enumerate(dirs):
            near = ring(second_axis[part] + d, 4)
            remote(
                r3.at[part, h], r3.at[part, h], s3_sem.at[part, h], r3_sem.at[part, h], s, f
            ).wait_recv()
            cols = slice(h * (PART // 2), (h + 1) * (PART // 2))
            second[part, near, :, cols] = (
                second[part, near, :, cols].astype(F32) + r3[part, h].astype(F32)
            ).astype(BF)
            copy = remote(
                second.at[part, near],
                r4.at[part, h],
                s4_sem.at[part, h],
                r4_sem.at[part, h],
                s,
                neighbour(part, 1, d),
            )
            copy.start()
            sent.append(copy)
    give.wait()
    gin_ref[...] = (gi[own_tok, :] + grecv[...].astype(F32)).astype(BF)
    for part in range(2):
        for h in range(2):
            remote(
                r4.at[part, h], r4.at[part, h], s4_sem.at[part, h], r4_sem.at[part, h], s, f
            ).wait_recv()
        summed = (
            second[part, second_axis[part]].astype(F32)
            + r4[part, 0].astype(F32)
            + r4[part, 1].astype(F32)
        ).astype(BF)
        for k in range(4):
            third[4 * part + k] = summed[:, k * HD : (k + 1) * HD]
    for step in range(1, NZ):
        chip = ring(z + step, NZ)
        copy = remote(
            third.at[chip], zr.at[step], zs_sem.at[step], zr_sem, 2 * chip + c, f
        )
        copy.start()
        sent.append(copy)
    for copy in sent:
        copy.wait_send()
    swap.wait_send()
    for step in range(1, NZ):
        d_copy(step)[1].wait_send()

    @pl.when(target != s)
    def _():
        copy0 = d_copy(0)[1]
        copy0.wait_send()

    keep_o.wait()
    others = o_ref.at[pl.ds(0, SEQLEN - TOK)]
    whole = remote(others, others, os_sem, or_sem, sib, f)
    whole.wait_send()
    whole.wait_recv()
    rest = zr.at[pl.ds(1, NZ - 1)]
    pltpu.make_async_copy(rest, rest, zr_sem).wait()
    acc = third[z].astype(F32)
    for step in range(1, NZ):
        acc = acc + zr[step].astype(F32)
    gw_ref[...] = acc


def k3(o, dkv, xt, wh, cosine, sine):
    dma = pltpu.SemaphoreType.DMA
    return pl.pallas_call(
        k3_kernel,
        out_shape=(
            jax.ShapeDtypeStruct((TOK, 2048), BF),
            jax.ShapeDtypeStruct((TOK, D), BF),
            jax.ShapeDtypeStruct((ROWS, HD), F32),
        ),
        in_specs=[ANY, ANY, VM, ANY, VM, VM],
        out_specs=(ANY, VM, VM),
        scratch_shapes=[
            pltpu.VMEM((D, HALF), BF),
            pltpu.VMEM((SEQLEN, HD), BF),
            pltpu.VMEM((SEQLEN, HD), BF),
            pltpu.VMEM((SEQLEN, HD), BF),
            pltpu.VMEM((8, CTOK, HD), BF),
            pltpu.VMEM((CTOK, HALF), BF),
            pltpu.VMEM((CTOK, D), F32),
            pltpu.VMEM((TOK, D), BF),
            pltpu.VMEM((TOK, D), BF),
            pltpu.VMEM((2, 4, 4, ROWS, PART), BF),
            pltpu.VMEM((2, 2, 4, ROWS, PART // 2), BF),
            pltpu.VMEM((2, 2, 4, ROWS, PART), BF),
            pltpu.VMEM((2, 4, ROWS, PART), BF),
            pltpu.VMEM((2, 2, ROWS, PART // 2), BF),
            pltpu.VMEM((2, 2, ROWS, PART), BF),
            pltpu.VMEM((8, ROWS, HD), BF),
            pltpu.VMEM((8, ROWS, HD), BF),
            dma((2,)),
            dma((2,)),
            dma((8,)),
            dma(()),
            dma(()),
            dma(()),
            dma(()),
            dma((2,)),
            dma((2, 2)),
            dma((2, 2)),
            dma((2, 2)),
            dma((2, 2)),
            dma((2, 2)),
            dma((2, 2)),
            dma((2, 2)),
            dma((2, 2)),
            dma((8,)),
            dma(()),
        ],
        compiler_params=pltpu.CompilerParams(
            collective_id=1, has_side_effects=True, vmem_limit_bytes=48 << 20
        ),
        name="gradients",
    )(o, dkv, xt, wh, cosine, sine)


def tables(lengths):
    z = lax.axis_index("seq") // 2
    places = z * CTOK + jnp.arange(CTOK, dtype=jnp.int32)
    order = jnp.arange(NDOC)
    doc_ends = jnp.sum(jnp.where(order[:, None] <= order[None, :], lengths[:, None], 0), axis=0)
    ended = doc_ends[None, :] <= places[:, None]
    within = places - jnp.sum(jnp.where(ended, lengths[None, :], 0), axis=1)
    exponent = jnp.arange(HD // 2, dtype=F32) * (2.0 / HD)
    rate = jnp.power(ROPE_BASE, -exponent)
    angles = within.astype(F32)[:, None] * rate[None, :]
    cosine, sine = jnp.cos(angles), jnp.sin(angles)
    return (
        jnp.concatenate([cosine, cosine], axis=1),
        jnp.concatenate([-sine, sine], axis=1),
    )


def on_device(inputs, queries, w_kv, doc_lengths, grad_out):
    cosine, sine = tables(doc_lengths[0])
    qh, gh, kv, xt, wh = k1(inputs[0], queries[0], w_kv, grad_out[0], cosine, sine)
    o, dkv = k2(doc_lengths[0], qh, gh, kv)
    out, gin, gw = k3(o, dkv, xt, wh, cosine, sine)
    return out[None], gin[None], gw


def solution(mesh):
    in_specs = (
        P("fsdp", "seq", None),
        P("fsdp", "seq", None),
        P("fsdp", None),
        P("fsdp", None),
        P("fsdp", "seq", None),
    )
    out_specs = (P("fsdp", "seq", None), P("fsdp", "seq", None), P("fsdp", "seq"))
    return jax.shard_map(
        on_device, mesh=mesh, in_specs=in_specs, out_specs=out_specs, check_vma=False
    )
```

time: 727 us -> 151 us (0.21)
  the two profiles are of different devices: /device:TPU:192 before, /device:TPU:2 now
where the time goes in v1:
time: 151 us
  Pallas kernels  139 us (92%)
  local copies, waits for them, and re-layouts  9.23 us (6%)
  other arithmetic  2.17 us (1%)
    pallas_call x1, Pallas kernels, k3(): pl.pallas_call(k3_kernel, out_shape=(jax.ShapeDtypeStruct((TOK, 2048), BF...  64.1 us
    pallas_call x1, Pallas kernels, k1(): pl.pallas_call(k1_kernel, out_shape=(seq_block, seq_block, jax.ShapeDtype...  50.4 us
    pallas_call x1, Pallas kernels, k2(): pl.pallas_call(k2_kernel, out_shape=(jax.ShapeDtypeStruct((SEQLEN, HD), B...  24.5 us
    unnamed x15, local copies, waits for them, and re-layouts  9.23 us

profile of v1, /device:TPU:2, one launch (start us, length us, event | category | flops | bytes accessed | tf_op | source)
XLA Modules:
  0.0 151.2 jit_solution(14827974670554068047)
XLA Ops:
  0.6 0.7 select_reduce_fusion.1
  1.4 0.7 select_reduce_fusion
  2.2 0.5 fusion
  2.7 0.1 pad_maximum_fusion
  2.8 0.0 copy-start.1
  2.9 1.1 copy-done.1
  3.9 0.0 copy-start.2
  3.9 1.1 copy-done.2
  5.0 0.0 copy-start.3
  5.0 1.0 copy-done.3
  6.0 0.0 copy-start.4
  6.0 1.0 copy-done.4
  7.1 50.4 %gather_project.1 = (bf16[2048,128]{1,0:T(8,128)(2,1)S(1)}, bf16[2048,128]{1,0:T(8,128)(2,1)S(1)}, bf16[2,2048,128]{2,1,0:T(8,128)(2,1)S(1)}, bf16[2304,256]{1,0:T(8,128)(2,1)S(1)}, bf16[2304,1024]{1,0:T(8,128)(2,1)S(1)}) custom-call(bf16[128,2304]{1,0:T(8,128)(2,1)S(1)} %bitcast.6, bf16[128,2048]{1,0:T(8,128)(2,1)S(1)} %bitcast.8, ...), custom_call_target="tpu_custom_call" | custom-call | tf_op jit(solution)/shard_map/gather_project/pallas_call | solution.py:275
  57.5 0.0 copy-start
  57.5 2.1 %copy-done = bf16[2304,1024]{1,0:T(8,128)(2,1)} copy-done((bf16[2304,1024]{1,0:T(8,128)(2,1)}, bf16[2304,1024]{1,0:T(8,128)(2,1)S(1)}, u32[]{:S(2)}) %copy-start) | copy-done | bytes 4718616
  59.6 0.0 copy-start.5
  59.6 0.7 copy-done.5
  60.3 24.5 %attend.1 = (bf16[2048,128]{1,0:T(8,128)(2,1)S(1)}, bf16[2,2048,128]{2,1,0:T(8,128)(2,1)S(1)}) custom-call(s32[8]{0:T(128)S(1)} %bitcast.13, bf16[2048,128]{1,0:T(8,128)(2,1)S(1)} %get-tuple-element.13.q_ref, bf16[2048,128]{1,0:T(8,128)(2,1)S(1)} %get-tuple-element.14.g_ref, bf16[2,2048,128]{2,1,0:T(8,128)(2,1)S(1)} %get-tuple-element.15.kv_ref), custom_call_target="tpu_custom_call" | custom-call | tf_op jit(solution)/shard_map/attend/pallas_call | solution.py:390
  84.8 64.1 %gradients.1 = (bf16[128,2048]{1,0:T(8,128)(2,1)S(1)}, bf16[128,2304]{1,0:T(8,128)(2,1)S(1)}, f32[144,128]{1,0:T(8,128)S(1)}) custom-call(bf16[2048,128]{1,0:T(8,128)(2,1)S(1)} %get-tuple-element.16.o_ref, bf16[2,2048,128]{2,1,0:T(8,128)(2,1)S(1)} %get-tuple-element.17.dkv_ref, bf16[2304,256]{1,0:T(8,128)(2,1)S(1)} %get-tuple-element.18.xt_ref, ...), custom_call_target="tpu_custom_call" | custom-call | tf_op jit(solution)/shard_map/gradients/pallas_call | solution.py:688
  148.9 0.8 copy.11
  149.7 0.8 copy.12
  150.6 0.6 copy.13
  (3 shorter events, 0.0 us)
Async XLA Ops:
  2.8 1.1 copy-start.1
  3.9 1.1 copy-start.2
  5.0 1.0 copy-start.3
  6.0 1.0 copy-start.4
  57.5 2.1 %copy-start = (bf16[2304,1024]{1,0:T(8,128)(2,1)}, bf16[2304,1024]{1,0:T(8,128)(2,1)S(1)}, u32[]{:S(2)}) copy-start(bf16[2304,1024]{1,0:T(8,128)(2,1)S(1)} %get-tuple-element.19.wh_ref) | copy-start | bytes 14155780
  59.6 0.7 copy-start.5

commit v2 on v1

v2 whole, which is shorter than its diff:
```python
import functools

import jax
import jax.numpy as jnp
from jax import lax
from jax.experimental import pallas as pl
from jax.experimental.pallas import tpu as pltpu
from jax.sharding import PartitionSpec as P

D = 2304
HD = 128
WIN = 1024
SEQLEN = 2048
NDOC = 8
NZ = 8
NX = 4
NY = 4
ROWS = D // (NX * NY)
HALF = 1024
PART = 512
TOK = 128
CTOK = 256
CAP = 50.0
SCALE = 1.0 / 12.0
ROPE_BASE = 10000.0
MESH = pl.DeviceIdType.MESH
HBM = pl.BlockSpec(memory_space=pltpu.HBM)
VM = pl.BlockSpec(memory_space=pltpu.VMEM)
BF = jnp.bfloat16
F32 = jnp.float32


def where_am_i():
    s = lax.axis_index("seq")
    f = lax.axis_index("fsdp")
    z = s // 2
    c = s - 2 * z
    x = f // NY
    y = f - NY * x
    return s, f, z, c, x, y


def ring(v, n):
    return lax.rem(v + n, n)


def remote(src, dst, send, recv, s, f):
    return pltpu.make_async_remote_copy(
        src_ref=src,
        dst_ref=dst,
        send_sem=send,
        recv_sem=recv,
        device_id={"seq": s, "fsdp": f},
        device_id_type=MESH,
    )


def enter(s, f, x, y):
    barrier = pltpu.get_barrier_semaphore()
    for step in range(1, 2 * NZ):
        pl.semaphore_signal(
            barrier,
            inc=1,
            device_id={"seq": ring(s + step, 2 * NZ), "fsdp": f},
            device_id_type=MESH,
        )
    for dx, dy in ((1, 0), (-1, 0), (0, 1), (0, -1)):
        pl.semaphore_signal(
            barrier,
            inc=1,
            device_id={"seq": s, "fsdp": ring(x + dx, NX) * NY + ring(y + dy, NY)},
            device_id_type=MESH,
        )
    pl.semaphore_wait(barrier, 2 * NZ - 1 + 4)


def rotated(values, cosine, sine):
    return values * cosine + pltpu.roll(values, HD // 2, 1) * sine


def k1_kernel(
    x_ref,
    q_ref,
    w_ref,
    g_ref,
    cos_ref,
    sin_ref,
    qh_ref,
    gh_ref,
    kv_ref,
    xs,
    wg,
    proj,
    wl_sem,
    xl_sem,
    xr_sem,
    ws_sem,
    wr_sem,
    ql_sem,
    qs_sem,
    qr_sem,
    ks_sem,
    kr_sem,
    fs_sem,
    fr_sem,
):
    s, f, z, c, x, y = where_am_i()
    sib = s + 1 - 2 * c
    own_rows = pl.ds(pl.multiple_of(f * ROWS, 16), ROWS)
    load_w = []
    for k in range(8):
        cols = pl.ds(pl.multiple_of((2 * k + c) * HD, HD), HD)
        load_w.append(
            pltpu.make_async_copy(
                w_ref.at[:, cols], wg.at[own_rows, pl.ds(k * HD, HD)], wl_sem.at[k]
            )
        )
    for copy in load_w:
        copy.start()
    own_tok = pl.ds(pl.multiple_of(c * TOK, TOK), TOK)
    load_x = pltpu.make_async_copy(x_ref, xs.at[own_tok], xl_sem)
    load_x.start()
    enter(s, f, x, y)

    wide = PART // 2

    def piece(phase, part, off, half):
        origin = ring(x + off[0], NX) * NY + ring(y + off[1], NY)
        rows = pl.ds(pl.multiple_of(origin * ROWS, 16), ROWS)
        base = phase * PART + part * wide
        if half is None:
            return wg.at[rows, pl.ds(base, wide)]
        return wg.at[rows, pl.ds(base + half * (wide // 2), wide // 2)]

    sends = []

    def pass_on(phase, part, off, step, half=None):
        there = tuple((o - d) % 4 for o, d in zip(off, step))
        there = tuple(-1 if t == 3 else t for t in there)
        ref = piece(phase, part, off, half)
        copy = remote(
            ref,
            ref,
            ws_sem.at[len(sends)],
            wr_sem.at[phase, part, there[0] + 1, there[1] + 1, half or 0],
            s,
            ring(x + step[0], NX) * NY + ring(y + step[1], NY),
        )
        copy.start()
        sends.append(copy)

    def arrived(phase, part, off, half=None):
        ref = piece(phase, part, off, half)
        sem = wr_sem.at[phase, part, off[0] + 1, off[1] + 1, half or 0]
        pltpu.make_async_copy(ref, ref, sem).wait()

    def at(part, a, b):
        return (a, b) if part == 0 else (b, a)

    def begin(p):
        for d in (1, -1):
            for part in range(2):
                pass_on(p, part, (0, 0), at(part, d, 0))
        for d in (1, -1):
            for part in range(2):
                pass_on(p, part, (0, 0), at(part, 0, d))

    def near_first(p):
        for d in (-1, 1):
            for part in range(2):
                arrived(p, part, at(part, d, 0))
                pass_on(p, part, at(part, d, 0), at(part, -d, 0), 0 if d < 0 else 1)
                for e in (1, -1):
                    pass_on(p, part, at(part, d, 0), at(part, 0, e))

    def near_second(p):
        for d in (-1, 1):
            for part in range(2):
                arrived(p, part, at(part, 0, d))
                pass_on(p, part, at(part, 0, d), at(part, 0, -d), 0 if d < 0 else 1)

    def far_first(p):
        for part in range(2):
            arrived(p, part, at(part, 2, 0), 0)
            arrived(p, part, at(part, 2, 0), 1)
            for e in (1, -1):
                pass_on(p, part, at(part, 2, 0), at(part, 0, e))

    def rest_second(p):
        for a in (-1, 1, 2):
            for d in (-1, 1):
                for part in range(2):
                    arrived(p, part, at(part, a, d))
                    pass_on(p, part, at(part, a, d), at(part, 0, -d), 0 if d < 0 else 1)

    def finish(p):
        for a in (0, -1, 1, 2):
            for part in range(2):
                arrived(p, part, at(part, a, 2), 0)
                arrived(p, part, at(part, a, 2), 1)

    def kv_copy(k):
        kind = k // 4
        to = 2 * (2 * (k % 4) + c) + z // 4
        rows = pl.ds(pl.multiple_of(z * CTOK, CTOK), CTOK)
        local = pltpu.make_async_copy(proj.at[k], kv_ref.at[kind, rows], kr_sem.at[kind])
        away = remote(proj.at[k], kv_ref.at[kind, rows], ks_sem.at[k], kr_sem.at[kind], to, f)
        return to == s, local, away

    def project(p):
        for t in (2 * p, 2 * p + 1):
            res = jnp.dot(xs[...], wg[:, t * 256 : (t + 1) * 256], preferred_element_type=F32)
            for j in range(2):
                k = 2 * t + j
                block = res[:, j * HD : (j + 1) * HD]
                if k < 4:
                    block = rotated(block, cos_ref[...], sin_ref[...])
                proj[k] = block.astype(BF)
                mine, local, away = kv_copy(k)

                @pl.when(mine)
                def _():
                    local.start()

                @pl.when(jnp.logical_not(mine))
                def _():
                    away.start()

    shares = []

    def share(p):
        half = kv_ref.at[p, pl.ds(pl.multiple_of(c * (SEQLEN // 2), SEQLEN // 2), SEQLEN // 2)]
        pltpu.make_async_copy(half, half, kr_sem.at[p]).wait()
        copy = remote(half, half, fs_sem.at[p], fr_sem.at[p], sib, f)
        copy.start()
        shares.append(copy)

    for copy in load_w:
        copy.wait()
    begin(0)
    load_x.wait()
    give_x = remote(xs.at[own_tok], xs.at[own_tok], xr_sem.at[0], xr_sem.at[1], sib, f)
    give_x.start()

    own_seq = pl.ds(pl.multiple_of(s * TOK, TOK), TOK)
    own_head = pl.ds(pl.multiple_of(s * HD, HD), HD)
    keep = []
    for i, (src, dst) in enumerate(((q_ref, qh_ref), (g_ref, gh_ref))):
        keep.append(pltpu.make_async_copy(src.at[:, own_head], dst.at[own_seq], ql_sem.at[i]))
        keep[-1].start()
    for step in range(1, 2 * NZ):
        to = ring(s + step, 2 * NZ)
        head = pl.ds(pl.multiple_of(to * HD, HD), HD)
        for i, (src, dst) in enumerate(((q_ref, qh_ref), (g_ref, gh_ref))):
            remote(src.at[:, head], dst.at[own_seq], qs_sem.at[i], qr_sem.at[i], to, f).start()

    near_first(0)
    near_second(0)
    far_first(0)
    rest_second(0)
    begin(1)
    finish(0)
    give_x.wait_recv()
    project(0)
    near_first(1)
    near_second(1)
    far_first(1)
    rest_second(1)
    finish(1)
    project(1)
    share(0)
    for copy in sends:
        copy.wait_send()
    give_x.wait_send()
    for copy in keep:
        copy.wait()
    for i, dst in enumerate((qh_ref, gh_ref)):
        others = dst.at[pl.ds(0, SEQLEN - TOK)]
        pltpu.make_async_copy(others, others, qs_sem.at[i]).wait()
        pltpu.make_async_copy(others, others, qr_sem.at[i]).wait()
    share(1)
    for k in range(8):
        mine, _, away = kv_copy(k)

        @pl.when(jnp.logical_not(mine))
        def _():
            away.wait_send()

    for copy in shares:
        copy.wait()


def k1(x, q, w, g, cosine, sine):
    dma = pltpu.SemaphoreType.DMA
    seq_block = jax.ShapeDtypeStruct((SEQLEN, HD), BF)
    return pl.pallas_call(
        k1_kernel,
        out_shape=(
            seq_block,
            seq_block,
            jax.ShapeDtypeStruct((2, SEQLEN, HD), BF),
            jax.ShapeDtypeStruct((CTOK, D), BF),
            jax.ShapeDtypeStruct((D, HALF), BF),
        ),
        in_specs=[HBM, HBM, HBM, HBM, VM, VM],
        out_specs=(VM, VM, VM, VM, VM),
        scratch_shapes=[
            pltpu.VMEM((8, CTOK, HD), BF),
            dma((8,)),
            dma(()),
            dma((2,)),
            dma((80,)),
            dma((2, 2, 4, 4, 2)),
            dma((2,)),
            dma((2,)),
            dma((2,)),
            dma((8,)),
            dma((2,)),
            dma((2,)),
            dma((2,)),
        ],
        compiler_params=pltpu.CompilerParams(
            collective_id=0, has_side_effects=True, vmem_limit_bytes=16 << 20
        ),
        name="gather_project",
    )(x, q, w, g, cosine, sine)


QT = 256
KT = 256
NT = (((1,), (1,)), ((), ()))


def k2_kernel(len_ref, q_ref, g_ref, kv_ref, o_ref, dkv_ref, vt, wbuf, tbuf, dk, dv):
    ends = []
    total = 0
    for i in range(NDOC):
        total = total + len_ref[i]
        ends.append(total)
    dk[...] = jnp.zeros_like(dk)
    dv[...] = jnp.zeros_like(dv)

    def flip(i, carry):
        rows = pl.ds(pl.multiple_of(i * KT, KT), KT)
        vt[:, rows] = kv_ref[1, rows, :].T
        return carry

    lax.fori_loop(0, SEQLEN // KT, flip, 0)

    def one_tile(i, carry):
        base = i * QT
        rows = pl.ds(pl.multiple_of(base, QT), QT)
        qt = q_ref[rows, :]
        gt = g_ref[rows, :]
        pos = base + lax.broadcasted_iota(jnp.int32, (1, QT), 1)
        start = jnp.zeros((1, QT), jnp.int32)
        first = jnp.int32(0)
        for end in ends:
            start = jnp.where(pos >= end, end, start)
            first = jnp.where(base >= end, end, first)
        low = jnp.maximum(start, pos - (WIN - 1))
        first = jnp.maximum(first, base - (WIN - 1)) // KT

        def forward(t, state):
            acc, norm = state
            krows = pl.ds(pl.multiple_of(t * KT, KT), KT)
            st = lax.dot_general(kv_ref[0, krows, :], qt, NT, preferred_element_type=F32)
            squashed = jnp.tanh(st * (SCALE / CAP))
            key = t * KT + lax.broadcasted_iota(jnp.int32, (KT, QT), 0)
            allowed = (key <= pos) & (key >= low)
            weight = jnp.where(allowed, jnp.exp(CAP * squashed), 0.0)
            slot = t - first
            wbuf[slot] = weight
            tbuf[slot] = squashed
            norm = norm + jnp.sum(weight, axis=0, keepdims=True)
            acc = acc + jnp.dot(vt[:, krows], weight.astype(BF), preferred_element_type=F32)
            return acc, norm

        acc, norm = lax.fori_loop(
            first, i + 1, forward, (jnp.zeros((HD, QT), F32), jnp.zeros((1, QT), F32))
        )
        inverse = 1.0 / norm
        out_t = (acc * inverse).astype(BF)
        out = out_t.astype(F32).T
        o_ref[rows, :] = out.astype(BF)
        delta = jnp.sum(gt.astype(F32).T * out_t.astype(F32), axis=0, keepdims=True)

        def backward(t, carry2):
            krows = pl.ds(pl.multiple_of(t * KT, KT), KT)
            slot = t - first
            probs = wbuf[slot] * inverse
            squashed = tbuf[slot]
            dprob = lax.dot_general(kv_ref[1, krows, :], gt, NT, preferred_element_type=F32)
            dscore = probs * (dprob - delta) * (1.0 - squashed * squashed)
            dk[krows, :] += jnp.dot(dscore.astype(BF), qt, preferred_element_type=F32)
            dv[krows, :] += jnp.dot(probs.astype(BF), gt, preferred_element_type=F32)
            return carry2

        lax.fori_loop(first, i + 1, backward, 0)
        return carry

    lax.fori_loop(0, SEQLEN // QT, one_tile, 0)
    dkv_ref[0] = (dk[...] * SCALE).astype(BF)
    dkv_ref[1] = dv[...].astype(BF)


def k2(lengths, qh, gh, kv):
    return pl.pallas_call(
        k2_kernel,
        out_shape=(
            jax.ShapeDtypeStruct((SEQLEN, HD), BF),
            jax.ShapeDtypeStruct((2, SEQLEN, HD), BF),
        ),
        in_specs=[pl.BlockSpec(memory_space=pltpu.SMEM), VM, VM, VM],
        out_specs=(VM, VM),
        scratch_shapes=[
            pltpu.VMEM((HD, SEQLEN), BF),
            pltpu.VMEM((5, KT, QT), F32),
            pltpu.VMEM((5, KT, QT), F32),
            pltpu.VMEM((SEQLEN, HD), F32),
            pltpu.VMEM((SEQLEN, HD), F32),
        ],
        compiler_params=pltpu.CompilerParams(vmem_limit_bytes=16 << 20),
        name="attend",
    )(lengths, qh, gh, kv)


def k3_kernel(
    o_ref,
    dkv_ref,
    xs_ref,
    wv,
    cos_ref,
    sin_ref,
    out_ref,
    gin_ref,
    gw_ref,
    xt,
    theirs,
    total,
    got,
    dd,
    gi,
    gsend,
    grecv,
    part_sum,
    r1,
    r2,
    second,
    r3,
    third,
    zr,
    sib_sem,
    ds_sem,
    dr_sem,
    ol_sem,
    os_sem,
    or_sem,
    g_sem,
    s1_sem,
    r1_sem,
    s2_sem,
    r2_sem,
    s3_sem,
    r3_sem,
    zs_sem,
    zr_sem,
):
    s, f, z, c, x, y = where_am_i()
    sib = s + 1 - 2 * c
    enter(s, f, x, y)
    part_seq = SEQLEN // 2
    swap = remote(
        dkv_ref.at[:, pl.ds(pl.multiple_of((1 - c) * part_seq, part_seq), part_seq)],
        theirs,
        sib_sem.at[0],
        sib_sem.at[1],
        sib,
        f,
    )
    swap.start()

    def turn(i, carry):
        cols = pl.ds(pl.multiple_of(i * 256, 256), 256)
        xt[cols, :] = xs_ref[:, cols].T
        return carry

    lax.fori_loop(0, D // 256, turn, 0)
    swap.wait_recv()

    def d_copy(kind, j):
        chip = 4 * c + j
        rows = pl.ds(j * CTOK, CTOK)
        to = 2 * chip + lax.rem(z, 2)
        slot = 4 * kind + z // 2
        src = total.at[kind, rows]
        local = pltpu.make_async_copy(src, got.at[slot], dr_sem.at[kind])
        away = remote(src, got.at[slot], ds_sem.at[kind, j], dr_sem.at[kind], to, f)
        return to == s, local, away

    def add_up(kind):
        for j in range(4):
            there = pl.ds(pl.multiple_of((4 * c + j) * CTOK, CTOK), CTOK)
            rows = pl.ds(j * CTOK, CTOK)
            total[kind, rows, :] = (
                dkv_ref[kind, there, :].astype(F32) + theirs[kind, rows, :].astype(F32)
            ).astype(BF)

    def send_out(kind):
        for j in range(4):
            mine, local, away = d_copy(kind, j)

            @pl.when(mine)
            def _():
                local.start()

            @pl.when(jnp.logical_not(mine))
            def _():
                away.start()

    def take_in(kind):
        blocks = got.at[pl.ds(4 * kind, 4)]
        pltpu.make_async_copy(blocks, blocks, dr_sem.at[kind]).wait()
        for k in range(4 * kind, 4 * kind + 4):
            block = got[k]
            if kind == 0:
                block = rotated(block.astype(F32), cos_ref[...], -sin_ref[...]).astype(BF)
            dd[:, k * HD : (k + 1) * HD] = block

    wide = PART // 2

    def chunk(p, part, a):
        cols = pl.ds(p * PART + part * wide, wide)
        for j in range(4):
            cx, cy = (a, j) if part == 0 else (j, a)
            rows = pl.ds(pl.multiple_of((cx * NY + cy) * ROWS, 16), ROWS)
            part_sum[p, part, cx, cy] = jnp.dot(
                xt[rows, :], dd[:, cols], preferred_element_type=F32
            ).astype(BF)

    def chunk_ref(p, part, a, cols):
        if part == 0:
            return part_sum.at[p, part, a, :, :, cols]
        return part_sum.at[p, part, :, a, :, cols]

    first_axis = (x, y)
    second_axis = (y, x)

    def neighbour(part, level, d):
        if (part == 0) == (level == 0):
            return ring(x + d, NX) * NY + y
        return x * NY + ring(y + d, NY)

    halves = (pl.ds(0, wide // 2), pl.ds(wide // 2, wide // 2))
    full = pl.ds(0, wide)
    dirs = (1, -1)
    sent = []

    def landed(ref, sem):
        pltpu.make_async_copy(ref, ref, sem).wait()

    def go(src, dst, send, recv, to_f):
        copy = remote(src, dst, send, recv, s, to_f)
        copy.start()
        sent.append(copy)

    def far(p):
        for part in range(2):
            a = ring(first_axis[part] + 2, 4)
            chunk(p, part, a)
            for h, d in enumerate(dirs):
                go(
                    chunk_ref(p, part, a, halves[h]),
                    r1.at[p, part, h],
                    s1_sem.at[p, part, h],
                    r1_sem.at[p, part, h],
                    neighbour(part, 0, d),
                )

    def near(p):
        for part in range(2):
            for d in (1, -1, 0):
                chunk(p, part, ring(first_axis[part] + d, 4))

    def hop(p):
        for h, d in enumerate(dirs):
            for part in range(2):
                a = ring(first_axis[part] + d, 4)
                landed(r1.at[p, part, h], r1_sem.at[p, part, h])
                cols = slice(h * (wide // 2), (h + 1) * (wide // 2))
                for j in range(4):
                    idx = (p, part, a, j) if part == 0 else (p, part, j, a)
                    idx = idx + (slice(None), cols)
                    part_sum[idx] = (
                        part_sum[idx].astype(F32) + r1[p, part, h, j].astype(F32)
                    ).astype(BF)
                go(
                    chunk_ref(p, part, a, full),
                    r2.at[p, part, h],
                    s2_sem.at[p, part, h],
                    r2_sem.at[p, part, h],
                    neighbour(part, 0, d),
                )

    def across(p):
        for part in range(2):
            for h in range(2):
                landed(r2.at[p, part, h], r2_sem.at[p, part, h])
            for j in range(4):
                idx = (p, part, x, j) if part == 0 else (p, part, j, y)
                second[p, part, j] = (
                    part_sum[idx].astype(F32)
                    + r2[p, part, 0, j].astype(F32)
                    + r2[p, part, 1, j].astype(F32)
                ).astype(BF)
            for i, d in enumerate((2, 1, -1)):
                go(
                    second.at[p, part, ring(second_axis[part] + d, 4)],
                    r3.at[p, part, i],
                    s3_sem.at[p, part, i],
                    r3_sem.at[p, part, i],
                    neighbour(part, 1, d),
                )

    def z_copy(p, j):
        chip = 4 * p + j
        return chip != z, remote(
            third.at[chip], zr.at[z], zs_sem.at[chip], zr_sem, 2 * chip + c, f
        )

    def along(p):
        for part in range(2):
            acc = second[p, part, second_axis[part]].astype(F32)
            for i in range(3):
                landed(r3.at[p, part, i], r3_sem.at[p, part, i])
                acc = acc + r3[p, part, i].astype(F32)
            for k in range(2):
                j = 2 * part + k
                third[4 * p + j] = acc[:, k * HD : (k + 1) * HD].astype(BF)
                away, copy = z_copy(p, j)

                @pl.when(away)
                def _():
                    copy.start()

    add_up(0)
    send_out(0)
    add_up(1)
    take_in(0)
    send_out(1)
    far(0)
    near(0)
    hop(0)
    take_in(1)
    own_head = pl.ds(pl.multiple_of(s * HD, HD), HD)
    own_seq = pl.ds(pl.multiple_of(s * TOK, TOK), TOK)
    keep_o = pltpu.make_async_copy(o_ref.at[own_seq], out_ref.at[:, own_head], ol_sem)
    far(1)
    keep_o.start()
    for step in range(1, 2 * NZ):
        to = ring(s + step, 2 * NZ)
        theirs_tok = pl.ds(pl.multiple_of(to * TOK, TOK), TOK)
        remote(
            o_ref.at[theirs_tok], out_ref.at[:, own_head], os_sem, or_sem, to, f
        ).start()
    near(1)
    across(0)
    hop(1)

    def input_tile(i, carry):
        rows = pl.ds(pl.multiple_of(i * 256, 256), 256)
        gi[:, rows] = lax.dot_general(dd[...], wv[rows, :], NT, preferred_element_type=F32)
        return carry

    lax.fori_loop(0, D // 256, input_tile, 0)
    other_tok = pl.ds(pl.multiple_of((1 - c) * TOK, TOK), TOK)
    own_tok = pl.ds(pl.multiple_of(c * TOK, TOK), TOK)
    gsend[...] = gi[other_tok, :].astype(BF)
    give = remote(gsend, grecv, g_sem.at[0], g_sem.at[1], sib, f)
    give.start()
    along(0)
    give.wait()
    gin_ref[...] = (gi[own_tok, :] + grecv[...].astype(F32)).astype(BF)
    across(1)
    along(1)
    for copy in sent:
        copy.wait_send()
    swap.wait_send()
    for kind in range(2):
        for j in range(4):
            mine, _, away = d_copy(kind, j)

            @pl.when(jnp.logical_not(mine))
            def _():
                away.wait_send()

    keep_o.wait()
    others = o_ref.at[pl.ds(0, SEQLEN - TOK)]
    landed(others, os_sem)
    landed(others, or_sem)
    for p in range(2):
        for j in range(4):
            away, copy = z_copy(p, j)

            @pl.when(away)
            def _():
                copy.wait_send()

    rest = zr.at[pl.ds(1, NZ - 1)]
    landed(rest, zr_sem)
    acc = third[z].astype(F32)
    for step in range(1, NZ):
        acc = acc + zr[ring(z + step, NZ)].astype(F32)
    gw_ref[...] = acc


def k3(o, dkv, xs, wh, cosine, sine):
    dma = pltpu.SemaphoreType.DMA
    wide = PART // 2
    return pl.pallas_call(
        k3_kernel,
        out_shape=(
            jax.ShapeDtypeStruct((TOK, 2048), BF),
            jax.ShapeDtypeStruct((TOK, D), BF),
            jax.ShapeDtypeStruct((ROWS, HD), F32),
        ),
        in_specs=[VM, VM, VM, VM, VM, VM],
        out_specs=(VM, VM, VM),
        scratch_shapes=[
            pltpu.VMEM((D, CTOK), BF),
            pltpu.VMEM((2, SEQLEN // 2, HD), BF),
            pltpu.VMEM((2, SEQLEN // 2, HD), BF),
            pltpu.VMEM((8, CTOK, HD), BF),
            pltpu.VMEM((CTOK, HALF), BF),
            pltpu.VMEM((CTOK, D), F32),
            pltpu.VMEM((TOK, D), BF),
            pltpu.VMEM((TOK, D), BF),
            pltpu.VMEM((2, 2, 4, 4, ROWS, wide), BF),
            pltpu.VMEM((2, 2, 2, 4, ROWS, wide // 2), BF),
            pltpu.VMEM((2, 2, 2, 4, ROWS, wide), BF),
            pltpu.VMEM((2, 2, 4, ROWS, wide), BF),
            pltpu.VMEM((2, 2, 3, ROWS, wide), BF),
            pltpu.VMEM((8, ROWS, HD), BF),
            pltpu.VMEM((8, ROWS, HD), BF),
            dma((2,)),
            dma((2, 4)),
            dma((2,)),
            dma(()),
            dma(()),
            dma(()),
            dma((2,)),
            dma((2, 2, 2)),
            dma((2, 2, 2)),
            dma((2, 2, 2)),
            dma((2, 2, 2)),
            dma((2, 2, 3)),
            dma((2, 2, 3)),
            dma((8,)),
            dma(()),
        ],
        compiler_params=pltpu.CompilerParams(
            collective_id=1, has_side_effects=True, vmem_limit_bytes=28 << 20
        ),
        name="gradients",
    )(o, dkv, xs, wh, cosine, sine)


def tables(lengths):
    z = lax.axis_index("seq") // 2
    places = z * CTOK + jnp.arange(CTOK, dtype=jnp.int32)
    order = jnp.arange(NDOC)
    doc_ends = jnp.sum(jnp.where(order[:, None] <= order[None, :], lengths[:, None], 0), axis=0)
    ended = doc_ends[None, :] <= places[:, None]
    within = places - jnp.sum(jnp.where(ended, lengths[None, :], 0), axis=1)
    exponent = jnp.arange(HD // 2, dtype=F32) * (2.0 / HD)
    rate = jnp.power(ROPE_BASE, -exponent)
    angles = within.astype(F32)[:, None] * rate[None, :]
    cosine, sine = jnp.cos(angles), jnp.sin(angles)
    return (
        jnp.concatenate([cosine, cosine], axis=1),
        jnp.concatenate([-sine, sine], axis=1),
    )


def on_device(inputs, queries, w_kv, doc_lengths, grad_out):
    cosine, sine = tables(doc_lengths[0])
    held = [
        pltpu.with_memory_space_constraint(a, pltpu.HBM)
        for a in (inputs[0], queries[0], w_kv, grad_out[0])
    ]
    qh, gh, kv, xs, wh = k1(*held, cosine, sine)
    o, dkv = k2(doc_lengths[0], qh, gh, kv)
    out, gin, gw = k3(o, dkv, xs, wh, cosine, sine)
    return out[None], gin[None], gw


def solution(mesh):
    in_specs = (
        P("fsdp", "seq", None),
        P("fsdp", "seq", None),
        P("fsdp", None),
        P("fsdp", None),
        P("fsdp", "seq", None),
    )
    out_specs = (P("fsdp", "seq", None), P("fsdp", "seq", None), P("fsdp", "seq"))
    return jax.shard_map(
        on_device, mesh=mesh, in_specs=in_specs, out_specs=out_specs, check_vma=False
    )
```

time: 151 us -> 137 us (0.907)
  the two profiles are of different devices: /device:TPU:2 before, /device:TPU:192 now
where the time goes in v2:
time: 137 us; the launch traced here: 135 us
  Pallas kernels  129 us (94%)
  local copies, waits for them, and re-layouts  2.89 us (2%)
  other arithmetic  2.17 us (2%)
    pallas_call x1, Pallas kernels, k3(): pl.pallas_call(k3_kernel, out_shape=(jax.ShapeDtypeStruct((TOK, 2048), BF...  52.8 us
    pallas_call x1, Pallas kernels, k1(): pl.pallas_call(k1_kernel, out_shape=(seq_block, seq_block, jax.ShapeDtype...  51.5 us
    pallas_call x1, Pallas kernels, k2(): pl.pallas_call(k2_kernel, out_shape=(jax.ShapeDtypeStruct((SEQLEN, HD), B...  24.4 us
    unnamed x5, local copies, waits for them, and re-layouts  2.89 us

profile of v2, /device:TPU:192, one launch (start us, length us, event | category | flops | bytes accessed | tf_op | source)
XLA Modules:
  0.0 134.6 jit_solution(4229436301924346514)
XLA Ops:
  0.6 0.7 select_reduce_fusion.1
  1.4 0.7 select_reduce_fusion
  2.2 0.5 fusion
  2.7 0.1 pad_maximum_fusion
  2.8 51.5 %gather_project.1 = (bf16[2048,128]{1,0:T(8,128)(2,1)S(1)}, bf16[2048,128]{1,0:T(8,128)(2,1)S(1)}, bf16[2,2048,128]{2,1,0:T(8,128)(2,1)S(1)}, bf16[256,2304]{1,0:T(8,128)(2,1)S(1)}, bf16[2304,1024]{1,0:T(8,128)(2,1)S(1)}) custom-call(bf16[128,2304]{1,0:T(8,128)(2,1)} %bitcast.11, bf16[128,2048]{1,0:T(8,128)(2,1)} %bitcast.12, bf16[144,2048]{1,0:T(8,128)(2,1)} %w_ref.1, ...), custom_call_target="tpu_custom_call" | custom-call | tf_op jit(solution)/shard_map/gather_project/pallas_call | solution.py:296
  54.4 0.0 copy-start
  54.4 0.6 copy-done
  55.0 24.4 %attend.1 = (bf16[2048,128]{1,0:T(8,128)(2,1)S(1)}, bf16[2,2048,128]{2,1,0:T(8,128)(2,1)S(1)}) custom-call(s32[8]{0:T(128)S(1)} %bitcast.10, bf16[2048,128]{1,0:T(8,128)(2,1)S(1)} %get-tuple-element.13.q_ref, bf16[2048,128]{1,0:T(8,128)(2,1)S(1)} %get-tuple-element.14.g_ref, bf16[2,2048,128]{2,1,0:T(8,128)(2,1)S(1)} %get-tuple-element.15.kv_ref), custom_call_target="tpu_custom_call" | custom-call | tf_op jit(solution)/shard_map/attend/pallas_call | solution.py:408
  79.5 52.8 %gradients.1 = (bf16[128,2048]{1,0:T(8,128)(2,1)S(1)}, bf16[128,2304]{1,0:T(8,128)(2,1)S(1)}, f32[144,128]{1,0:T(8,128)S(1)}) custom-call(bf16[2048,128]{1,0:T(8,128)(2,1)S(1)} %get-tuple-element.16.o_ref, bf16[2,2048,128]{2,1,0:T(8,128)(2,1)S(1)} %get-tuple-element.17.dkv_ref, bf16[256,2304]{1,0:T(8,128)(2,1)S(1)} %get-tuple-element.18.xs_ref, ...), custom_call_target="tpu_custom_call" | custom-call | tf_op jit(solution)/shard_map/gradients/pallas_call | solution.py:720
  132.3 0.8 copy.11
  133.1 0.8 copy.12
  133.9 0.6 copy.13
  (3 shorter events, 0.0 us)
Async XLA Ops:
  54.4 0.7 copy-start

commit v3 on v2

--- a/solution.py
+++ b/solution.py
@@ -255,16 +255,16 @@
             remote(src.at[:, head], dst.at[own_seq], qs_sem.at[i], qr_sem.at[i], to, f).start()
 
     near_first(0)
+    begin(1)
     near_second(0)
     far_first(0)
+    near_first(1)
     rest_second(0)
-    begin(1)
+    near_second(1)
+    far_first(1)
     finish(0)
     give_x.wait_recv()
     project(0)
-    near_first(1)
-    near_second(1)
-    far_first(1)
     rest_second(1)
     finish(1)
     project(1)
@@ -331,6 +331,9 @@
 NT = (((1,), (1,)), ((), ()))
 
 
+LOG2E = 1.4426950408889634
+
+
 def k2_kernel(len_ref, q_ref, g_ref, kv_ref, o_ref, dkv_ref, vt, wbuf, tbuf, dk, dv):
     ends = []
     total = 0
@@ -350,8 +353,6 @@
     def one_tile(i, carry):
         base = i * QT
         rows = pl.ds(pl.multiple_of(base, QT), QT)
-        qt = q_ref[rows, :]
-        gt = g_ref[rows, :]
         pos = base + lax.broadcasted_iota(jnp.int32, (1, QT), 1)
         start = jnp.zeros((1, QT), jnp.int32)
         first = jnp.int32(0)
@@ -360,43 +361,47 @@
             first = jnp.where(base >= end, end, first)
         low = jnp.maximum(start, pos - (WIN - 1))
         first = jnp.maximum(first, base - (WIN - 1)) // KT
-
-        def forward(t, state):
-            acc, norm = state
-            krows = pl.ds(pl.multiple_of(t * KT, KT), KT)
-            st = lax.dot_general(kv_ref[0, krows, :], qt, NT, preferred_element_type=F32)
-            squashed = jnp.tanh(st * (SCALE / CAP))
-            key = t * KT + lax.broadcasted_iota(jnp.int32, (KT, QT), 0)
-            allowed = (key <= pos) & (key >= low)
-            weight = jnp.where(allowed, jnp.exp(CAP * squashed), 0.0)
-            slot = t - first
-            wbuf[slot] = weight
-            tbuf[slot] = squashed
-            norm = norm + jnp.sum(weight, axis=0, keepdims=True)
-            acc = acc + jnp.dot(vt[:, krows], weight.astype(BF), preferred_element_type=F32)
-            return acc, norm
-
-        acc, norm = lax.fori_loop(
-            first, i + 1, forward, (jnp.zeros((HD, QT), F32), jnp.zeros((1, QT), F32))
-        )
-        inverse = 1.0 / norm
-        out_t = (acc * inverse).astype(BF)
-        out = out_t.astype(F32).T
-        o_ref[rows, :] = out.astype(BF)
-        delta = jnp.sum(gt.astype(F32).T * out_t.astype(F32), axis=0, keepdims=True)
-
-        def backward(t, carry2):
-            krows = pl.ds(pl.multiple_of(t * KT, KT), KT)
-            slot = t - first
-            probs = wbuf[slot] * inverse
-            squashed = tbuf[slot]
-            dprob = lax.dot_general(kv_ref[1, krows, :], gt, NT, preferred_element_type=F32)
-            dscore = probs * (dprob - delta) * (1.0 - squashed * squashed)
-            dk[krows, :] += jnp.dot(dscore.astype(BF), qt, preferred_element_type=F32)
-            dv[krows, :] += jnp.dot(probs.astype(BF), gt, preferred_element_type=F32)
-            return carry2
-
-        lax.fori_loop(first, i + 1, backward, 0)
+        count = i + 1 - first
+        for n in range(1, 6):
+
+            @pl.when(count == n)
+            def _():
+                qt = q_ref[rows, :]
+                gt = g_ref[rows, :]
+                acc = jnp.zeros((HD, QT), F32)
+                norm = jnp.zeros((1, QT), F32)
+                key = lax.broadcasted_iota(jnp.int32, (KT, QT), 0)
+                spans = []
+                for j in range(n):
+                    spans.append(pl.ds(pl.multiple_of((first + j) * KT, KT), KT))
+                for j in range(n):
+                    st = lax.dot_general(
+                        kv_ref[0, spans[j], :], qt, NT, preferred_element_type=F32
+                    )
+                    squashed = jnp.tanh(st * (SCALE / CAP))
+                    allowed = key >= low - (first + j) * KT
+                    if j == n - 1:
+                        allowed = allowed & (key <= pos - (first + j) * KT)
+                    weight = jnp.where(allowed, jnp.exp2((CAP * LOG2E) * squashed), 0.0)
+                    short = weight.astype(BF)
+                    norm = norm + jnp.sum(weight, axis=0, keepdims=True)
+                    wbuf[j] = weight * (1.0 - squashed * squashed)
+                    tbuf[j] = short
+                    acc = acc + jnp.dot(vt[:, spans[j]], short, preferred_element_type=F32)
+                inverse = 1.0 / norm
+                out_t = (acc * inverse).astype(BF)
+                o_ref[rows, :] = out_t.T
+                gt_t = gt.astype(F32).T
+                delta = jnp.sum(gt_t * out_t.astype(F32), axis=0, keepdims=True)
+                scaled = (gt_t * inverse).T.astype(BF)
+                for j in range(n):
+                    dprob = lax.dot_general(
+                        kv_ref[1, spans[j], :], gt, NT, preferred_element_type=F32
+                    )
+                    dscore = (wbuf[j] * inverse * (dprob - delta)).astype(BF)
+                    dk[spans[j], :] += jnp.dot(dscore, qt, preferred_element_type=F32)
+                    dv[spans[j], :] += jnp.dot(tbuf[j], scaled, preferred_element_type=F32)
+
         return carry
 
     lax.fori_loop(0, SEQLEN // QT, one_tile, 0)
@@ -416,7 +421,7 @@
         scratch_shapes=[
             pltpu.VMEM((HD, SEQLEN), BF),
             pltpu.VMEM((5, KT, QT), F32),
-            pltpu.VMEM((5, KT, QT), F32),
+            pltpu.VMEM((5, KT, QT), BF),
             pltpu.VMEM((SEQLEN, HD), F32),
             pltpu.VMEM((SEQLEN, HD), F32),
         ],

time: 137 us -> 122 us (0.89)
  Pallas kernels: 129 us -> 115 us
    pallas_call x1, Pallas kernels: 24.4 us -> 13 us  [k2(): pl.pallas_call(k2_kernel, out_shape=(jax.ShapeDtypeStruct((SEQLEN, HD), B...]
    pallas_call x1, Pallas kernels: 51.5 us -> 48.1 us  [k1(): pl.pallas_call(k1_kernel, out_shape=(seq_block, seq_block, jax.ShapeDtype...]
where the time goes in v3:
time: 122 us; the launch traced here: 121 us
  Pallas kernels  115 us (94%)
  local copies, waits for them, and re-layouts  2.89 us (2%)
  other arithmetic  2.17 us (2%)
    pallas_call x1, Pallas kernels, k3(): pl.pallas_call(k3_kernel, out_shape=(jax.ShapeDtypeStruct((TOK, 2048), BF...  54 us
    pallas_call x1, Pallas kernels, k1(): pl.pallas_call(k1_kernel, out_shape=(seq_block, seq_block, jax.ShapeDtype...  48.1 us
    pallas_call x1, Pallas kernels, k2(): pl.pallas_call(k2_kernel, out_shape=(jax.ShapeDtypeStruct((SEQLEN, HD), B...  13 us
    unnamed x5, local copies, waits for them, and re-layouts  2.89 us

profile of v3, /device:TPU:192, one launch (start us, length us, event | category | flops | bytes accessed | tf_op | source)
XLA Modules:
  0.0 120.9 jit_solution(1789032725222779436)
XLA Ops:
  0.6 0.7 select_reduce_fusion.1
  1.4 0.7 select_reduce_fusion
  2.2 0.5 fusion
  2.7 0.1 pad_maximum_fusion
  2.8 48.1 %gather_project.1 = (bf16[2048,128]{1,0:T(8,128)(2,1)S(1)}, bf16[2048,128]{1,0:T(8,128)(2,1)S(1)}, bf16[2,2048,128]{2,1,0:T(8,128)(2,1)S(1)}, bf16[256,2304]{1,0:T(8,128)(2,1)S(1)}, bf16[2304,1024]{1,0:T(8,128)(2,1)S(1)}) custom-call(bf16[128,2304]{1,0:T(8,128)(2,1)} %bitcast.11, bf16[128,2048]{1,0:T(8,128)(2,1)} %bitcast.12, bf16[144,2048]{1,0:T(8,128)(2,1)} %w_ref.1, ...), custom_call_target="tpu_custom_call" | custom-call | tf_op jit(solution)/shard_map/gather_project/pallas_call | solution.py:296
  50.9 0.0 copy-start
  50.9 0.6 copy-done
  51.6 13.0 %attend.1 = (bf16[2048,128]{1,0:T(8,128)(2,1)S(1)}, bf16[2,2048,128]{2,1,0:T(8,128)(2,1)S(1)}) custom-call(s32[8]{0:T(128)S(1)} %bitcast.10, bf16[2048,128]{1,0:T(8,128)(2,1)S(1)} %get-tuple-element.13.q_ref, bf16[2048,128]{1,0:T(8,128)(2,1)S(1)} %get-tuple-element.14.g_ref, bf16[2,2048,128]{2,1,0:T(8,128)(2,1)S(1)} %get-tuple-element.15.kv_ref), custom_call_target="tpu_custom_call" | custom-call | tf_op jit(solution)/shard_map/attend/pallas_call | solution.py:413
  64.6 54.0 %gradients.1 = (bf16[128,2048]{1,0:T(8,128)(2,1)S(1)}, bf16[128,2304]{1,0:T(8,128)(2,1)S(1)}, f32[144,128]{1,0:T(8,128)S(1)}) custom-call(bf16[2048,128]{1,0:T(8,128)(2,1)S(1)} %get-tuple-element.16.o_ref, bf16[2,2048,128]{2,1,0:T(8,128)(2,1)S(1)} %get-tuple-element.17.dkv_ref, bf16[256,2304]{1,0:T(8,128)(2,1)S(1)} %get-tuple-element.18.xs_ref, ...), custom_call_target="tpu_custom_call" | custom-call | tf_op jit(solution)/shard_map/gradients/pallas_call | solution.py:725
  118.6 0.8 copy.11
  119.4 0.8 copy.12
  120.2 0.6 copy.13
  (3 shorter events, 0.0 us)
Async XLA Ops:
  50.9 0.7 copy-start

commit v4 on v3

v4 whole, which is shorter than its diff:
```python
import functools

import jax
import jax.numpy as jnp
from jax import lax
from jax.experimental import pallas as pl
from jax.experimental.pallas import tpu as pltpu
from jax.sharding import PartitionSpec as P

D = 2304
HD = 128
WIN = 1024
SEQLEN = 2048
NDOC = 8
NZ = 8
NX = 4
NY = 4
ROWS = D // (NX * NY)
HALF = 1024
PART = 512
TOK = 128
CTOK = 256
CAP = 50.0
SCALE = 1.0 / 12.0
ROPE_BASE = 10000.0
MESH = pl.DeviceIdType.MESH
HBM = pl.BlockSpec(memory_space=pltpu.HBM)
VM = pl.BlockSpec(memory_space=pltpu.VMEM)
BF = jnp.bfloat16
F32 = jnp.float32


def where_am_i():
    s = lax.axis_index("seq")
    f = lax.axis_index("fsdp")
    z = s // 2
    c = s - 2 * z
    x = f // NY
    y = f - NY * x
    return s, f, z, c, x, y


def ring(v, n):
    return lax.rem(v + n, n)


def remote(src, dst, send, recv, s, f):
    return pltpu.make_async_remote_copy(
        src_ref=src,
        dst_ref=dst,
        send_sem=send,
        recv_sem=recv,
        device_id={"seq": s, "fsdp": f},
        device_id_type=MESH,
    )


def enter(s, f, x, y):
    barrier = pltpu.get_barrier_semaphore()
    for step in range(1, 2 * NZ):
        pl.semaphore_signal(
            barrier,
            inc=1,
            device_id={"seq": ring(s + step, 2 * NZ), "fsdp": f},
            device_id_type=MESH,
        )
    for dx, dy in ((1, 0), (-1, 0), (0, 1), (0, -1)):
        pl.semaphore_signal(
            barrier,
            inc=1,
            device_id={"seq": s, "fsdp": ring(x + dx, NX) * NY + ring(y + dy, NY)},
            device_id_type=MESH,
        )
    pl.semaphore_wait(barrier, 2 * NZ - 1 + 4)


def other_chip(s, z):
    return s + 2 - 4 * lax.rem(z, 2)


def rotated(values, cosine, sine):
    return values * cosine + pltpu.roll(values, HD // 2, 1) * sine


def k1_kernel(
    x_ref,
    q_ref,
    w_ref,
    g_ref,
    cos_ref,
    sin_ref,
    qh_ref,
    gh_ref,
    kv_ref,
    xt_ref,
    xp_ref,
    wg,
    xs,
    xp,
    proj,
    wl_sem,
    xl_sem,
    xr_sem,
    xp_sem,
    ws_sem,
    wr_sem,
    ql_sem,
    qs_sem,
    qr_sem,
    ks_sem,
    kr_sem,
    fs_sem,
    fr_sem,
):
    s, f, z, c, x, y = where_am_i()
    sib = s + 1 - 2 * c
    own_rows = pl.ds(pl.multiple_of(f * ROWS, 16), ROWS)
    load_w = []
    for k in range(8):
        cols = pl.ds(pl.multiple_of((2 * k + c) * HD, HD), HD)
        load_w.append(
            pltpu.make_async_copy(
                w_ref.at[:, cols], wg.at[own_rows, pl.ds(k * HD, HD)], wl_sem.at[k]
            )
        )
    for copy in load_w:
        copy.start()
    own_tok = pl.ds(pl.multiple_of(c * TOK, TOK), TOK)
    load_x = pltpu.make_async_copy(x_ref, xs.at[own_tok], xl_sem)
    load_x.start()
    enter(s, f, x, y)

    wide = PART // 2

    def piece(phase, part, off, half):
        origin = ring(x + off[0], NX) * NY + ring(y + off[1], NY)
        rows = pl.ds(pl.multiple_of(origin * ROWS, 16), ROWS)
        base = phase * PART + part * wide
        if half is None:
            return wg.at[rows, pl.ds(base, wide)]
        return wg.at[rows, pl.ds(base + half * (wide // 2), wide // 2)]

    sends = []

    def pass_on(phase, part, off, step, half=None):
        there = tuple((o - d) % 4 for o, d in zip(off, step))
        there = tuple(-1 if t == 3 else t for t in there)
        ref = piece(phase, part, off, half)
        copy = remote(
            ref,
            ref,
            ws_sem.at[len(sends)],
            wr_sem.at[phase, part, there[0] + 1, there[1] + 1, half or 0],
            s,
            ring(x + step[0], NX) * NY + ring(y + step[1], NY),
        )
        copy.start()
        sends.append(copy)

    def arrived(phase, part, off, half=None):
        ref = piece(phase, part, off, half)
        sem = wr_sem.at[phase, part, off[0] + 1, off[1] + 1, half or 0]
        pltpu.make_async_copy(ref, ref, sem).wait()

    def at(part, a, b):
        return (a, b) if part == 0 else (b, a)

    def begin(p):
        for d in (1, -1):
            for part in range(2):
                pass_on(p, part, (0, 0), at(part, d, 0))
        for d in (1, -1):
            for part in range(2):
                pass_on(p, part, (0, 0), at(part, 0, d))

    def near_first(p):
        for d in (-1, 1):
            for part in range(2):
                arrived(p, part, at(part, d, 0))
                pass_on(p, part, at(part, d, 0), at(part, -d, 0), 0 if d < 0 else 1)
                for e in (1, -1):
                    pass_on(p, part, at(part, d, 0), at(part, 0, e))

    def near_second(p):
        for d in (-1, 1):
            for part in range(2):
                arrived(p, part, at(part, 0, d))
                pass_on(p, part, at(part, 0, d), at(part, 0, -d), 0 if d < 0 else 1)

    def far_first(p):
        for part in range(2):
            arrived(p, part, at(part, 2, 0), 0)
            arrived(p, part, at(part, 2, 0), 1)
            for e in (1, -1):
                pass_on(p, part, at(part, 2, 0), at(part, 0, e))

    def rest_second(p):
        for a in (-1, 1, 2):
            for d in (-1, 1):
                for part in range(2):
                    arrived(p, part, at(part, a, d))
                    pass_on(p, part, at(part, a, d), at(part, 0, -d), 0 if d < 0 else 1)

    def finish(p):
        for a in (0, -1, 1, 2):
            for part in range(2):
                arrived(p, part, at(part, a, 2), 0)
                arrived(p, part, at(part, a, 2), 1)

    def kv_copy(k):
        kind = k // 4
        to = 2 * (2 * (k % 4) + c) + z // 4
        rows = pl.ds(pl.multiple_of(z * CTOK, CTOK), CTOK)
        local = pltpu.make_async_copy(proj.at[k], kv_ref.at[kind, rows], kr_sem.at[kind])
        away = remote(proj.at[k], kv_ref.at[kind, rows], ks_sem.at[k], kr_sem.at[kind], to, f)
        return to == s, local, away

    in_pair = pl.ds(pl.multiple_of(lax.rem(z, 2) * CTOK, CTOK), CTOK)

    def project(p):
        for t in (2 * p, 2 * p + 1):
            res = jnp.dot(xs[...], wg[:, t * 256 : (t + 1) * 256], preferred_element_type=F32)
            for j in range(2):
                k = 2 * t + j
                block = res[:, j * HD : (j + 1) * HD]
                if k < 4:
                    block = rotated(block, cos_ref[in_pair, :], sin_ref[in_pair, :])
                proj[k] = block.astype(BF)
                mine, local, away = kv_copy(k)

                @pl.when(mine)
                def _():
                    local.start()

                @pl.when(jnp.logical_not(mine))
                def _():
                    away.start()

    shares = []

    def share(p):
        half = kv_ref.at[p, pl.ds(pl.multiple_of(c * (SEQLEN // 2), SEQLEN // 2), SEQLEN // 2)]
        pltpu.make_async_copy(half, half, kr_sem.at[p]).wait()
        copy = remote(half, half, fs_sem.at[p], fr_sem.at[p], sib, f)
        copy.start()
        shares.append(copy)

    for copy in load_w:
        copy.wait()
    begin(0)
    load_x.wait()
    give_x = remote(xs.at[own_tok], xs.at[own_tok], xr_sem.at[0], xr_sem.at[1], sib, f)
    give_x.start()

    own_seq = pl.ds(pl.multiple_of(s * TOK, TOK), TOK)
    own_head = pl.ds(pl.multiple_of(s * HD, HD), HD)
    keep = []
    for i, (src, dst) in enumerate(((q_ref, qh_ref), (g_ref, gh_ref))):
        keep.append(pltpu.make_async_copy(src.at[:, own_head], dst.at[own_seq], ql_sem.at[i]))
        keep[-1].start()
    for step in range(1, 2 * NZ):
        to = ring(s + step, 2 * NZ)
        head = pl.ds(pl.multiple_of(to * HD, HD), HD)
        for i, (src, dst) in enumerate(((q_ref, qh_ref), (g_ref, gh_ref))):
            remote(src.at[:, head], dst.at[own_seq], qs_sem.at[i], qr_sem.at[i], to, f).start()
    cross = remote(
        xs.at[own_tok, pl.ds(0, D // 2)],
        xp.at[own_tok],
        xp_sem.at[0],
        xp_sem.at[1],
        other_chip(s, z),
        f,
    )
    cross.start()

    near_first(0)
    begin(1)
    near_second(0)
    far_first(0)
    near_first(1)
    rest_second(0)
    near_second(1)
    far_first(1)
    finish(0)
    give_x.wait_recv()
    project(0)
    cross.wait_recv()
    spread = remote(xp.at[own_tok], xp.at[own_tok], xp_sem.at[2], xp_sem.at[3], sib, f)
    spread.start()
    rest_second(1)
    finish(1)
    project(1)
    share(0)

    def turn(i, carry):
        cols = pl.ds(pl.multiple_of(i * 256, 256), 256)
        xt_ref[cols, :] = xs[:, cols].T
        return carry

    def turn_half(i, carry):
        cols = pl.ds(pl.multiple_of(i * 128, 128), 128)
        xp_ref[cols, :] = xp[:, cols].T
        return carry

    lax.fori_loop(0, D // 256, turn, 0)
    spread.wait()
    cross.wait_send()
    lax.fori_loop(0, D // 256, turn_half, 0)
    for copy in sends:
        copy.wait_send()
    give_x.wait_send()
    for copy in keep:
        copy.wait()
    for i, dst in enumerate((qh_ref, gh_ref)):
        others = dst.at[pl.ds(0, SEQLEN - TOK)]
        pltpu.make_async_copy(others, others, qs_sem.at[i]).wait()
        pltpu.make_async_copy(others, others, qr_sem.at[i]).wait()
    share(1)
    for k in range(8):
        mine, _, away = kv_copy(k)

        @pl.when(jnp.logical_not(mine))
        def _():
            away.wait_send()

    for copy in shares:
        copy.wait()


def k1(x, q, w, g, cosine, sine):
    dma = pltpu.SemaphoreType.DMA
    seq_block = jax.ShapeDtypeStruct((SEQLEN, HD), BF)
    return pl.pallas_call(
        k1_kernel,
        out_shape=(
            seq_block,
            seq_block,
            jax.ShapeDtypeStruct((2, SEQLEN, HD), BF),
            jax.ShapeDtypeStruct((D, CTOK), BF),
            jax.ShapeDtypeStruct((D // 2, CTOK), BF),
            jax.ShapeDtypeStruct((D, HALF), BF),
        ),
        in_specs=[HBM, HBM, HBM, HBM, VM, VM],
        out_specs=(VM, VM, VM, VM, VM, VM),
        scratch_shapes=[
            pltpu.VMEM((CTOK, D), BF),
            pltpu.VMEM((CTOK, D // 2), BF),
            pltpu.VMEM((8, CTOK, HD), BF),
            dma((8,)),
            dma(()),
            dma((2,)),
            dma((4,)),
            dma((80,)),
            dma((2, 2, 4, 4, 2)),
            dma((2,)),
            dma((2,)),
            dma((2,)),
            dma((8,)),
            dma((2,)),
            dma((2,)),
            dma((2,)),
        ],
        compiler_params=pltpu.CompilerParams(
            collective_id=0, has_side_effects=True, vmem_limit_bytes=16 << 20
        ),
        name="gather_project",
    )(x, q, w, g, cosine, sine)


QT = 256
KT = 256
NT = (((1,), (1,)), ((), ()))
LOG2E = 1.4426950408889634


def k3_kernel(
    len_ref,
    q_ref,
    g_ref,
    kv_ref,
    xt,
    xp1,
    wv,
    cos_ref,
    sin_ref,
    out_ref,
    gin_ref,
    gw_ref,
    vt,
    wbuf,
    tbuf,
    dk,
    dv,
    obuf,
    dkv,
    theirs,
    total,
    got,
    dd,
    da,
    xp,
    gi,
    gsend,
    grecv,
    part_sum,
    r1,
    r2,
    second,
    r3,
    third,
    zr,
    x_sem,
    ws_sem,
    wr_sem,
    ds_sem,
    dr_sem,
    ol_sem,
    os_sem,
    or_sem,
    as_sem,
    ar_sem,
    g_sem,
    s1_sem,
    r1_sem,
    s2_sem,
    r2_sem,
    s3_sem,
    r3_sem,
    zs_sem,
    zr_sem,
):
    s, f, z, c, x, y = where_am_i()
    sib = s + 1 - 2 * c
    e = lax.rem(z, 2)
    pair = z // 2
    partner = other_chip(s, z)
    half_d = D // 2
    keep_x = pltpu.make_async_copy(xp1, xp.at[pl.ds(0, half_d)], x_sem.at[0])
    keep_x.start()
    enter(s, f, x, y)

    def landed(ref, sem):
        pltpu.make_async_copy(ref, ref, sem).wait()

    own_cols = pl.ds(pl.multiple_of(c * TOK, TOK), TOK)
    cross = remote(
        xt.at[pl.ds(half_d, half_d), own_cols],
        xp.at[pl.ds(half_d, half_d), own_cols],
        x_sem.at[1],
        x_sem.at[2],
        partner,
        f,
    )
    cross.start()
    spread = remote(
        xp.at[pl.ds(half_d, half_d), own_cols],
        xp.at[pl.ds(half_d, half_d), own_cols],
        x_sem.at[3],
        x_sem.at[4],
        sib,
        f,
    )

    ends = []
    so_far = 0
    for i in range(NDOC):
        so_far = so_far + len_ref[i]
        ends.append(so_far)
    dk[...] = jnp.zeros_like(dk)
    dv[...] = jnp.zeros_like(dv)

    def flip(i, carry):
        rows = pl.ds(pl.multiple_of(i * KT, KT), KT)
        vt[:, rows] = kv_ref[1, rows, :].T
        return carry

    lax.fori_loop(0, SEQLEN // KT, flip, 0)

    def tile_rows(i):
        return pl.ds(pl.multiple_of(i * KT, KT), KT)

    def swap(i):
        rows = tile_rows(i)
        return remote(
            dkv.at[1 - c, rows], theirs.at[rows], ws_sem.at[i], wr_sem.at[i], sib, f
        )

    def attend(i, n):
        base = i * QT
        rows = tile_rows(i)
        pos = base + lax.broadcasted_iota(jnp.int32, (1, QT), 1)
        start = jnp.zeros((1, QT), jnp.int32)
        for end in ends:
            start = jnp.where(pos >= end, end, start)
        low = jnp.maximum(start, pos - (WIN - 1))
        first = i + 1 - n
        qt = q_ref[rows, :]
        gt = g_ref[rows, :]
        acc = jnp.zeros((HD, QT), F32)
        norm = jnp.zeros((1, QT), F32)
        key = lax.broadcasted_iota(jnp.int32, (KT, QT), 0)
        spans = [tile_rows(first + j) for j in range(n)]
        for j in range(n):
            st = lax.dot_general(kv_ref[0, spans[j], :], qt, NT, preferred_element_type=F32)
            squashed = jnp.tanh(st * (SCALE / CAP))
            allowed = key >= low - (first + j) * KT
            if j == n - 1:
                allowed = allowed & (key <= pos - (first + j) * KT)
            weight = jnp.where(allowed, jnp.exp2((CAP * LOG2E) * squashed), 0.0)
            short = weight.astype(BF)
            norm = norm + jnp.sum(weight, axis=0, keepdims=True)
            wbuf[j] = weight * (1.0 - squashed * squashed)
            tbuf[j] = short
            acc = acc + jnp.dot(vt[:, spans[j]], short, preferred_element_type=F32)
        inverse = 1.0 / norm
        out_t = (acc * inverse).astype(BF)
        obuf[rows, :] = out_t.T
        gt_t = gt.astype(F32).T
        delta = jnp.sum(gt_t * out_t.astype(F32), axis=0, keepdims=True)
        scaled = (gt_t * inverse).T.astype(BF)
        for j in range(n):
            dprob = lax.dot_general(kv_ref[1, spans[j], :], gt, NT, preferred_element_type=F32)
            dscore = (wbuf[j] * inverse * (dprob - delta)).astype(BF)
            dk[spans[j], :] += jnp.dot(dscore, qt, preferred_element_type=F32)
            dv[spans[j], :] += jnp.dot(tbuf[j], scaled, preferred_element_type=F32)
        dkv[0, rows, :] = (dk[rows, :] * SCALE).astype(BF)
        dkv[1, rows, :] = dv[rows, :].astype(BF)
        swap(i).start()

    head_dev = lax.rem(z, 4)

    def d_copy(i):
        rows = tile_rows(i)
        to = 4 * (i // 2) + head_dev
        dst = got.at[2 * c + z // 4, pl.ds(pl.multiple_of(lax.rem(i, 2) * CTOK, CTOK), CTOK)]
        local = pltpu.make_async_copy(total.at[rows], dst, dr_sem.at[c])
        away = remote(total.at[rows], dst, ds_sem.at[i], dr_sem.at[c], to, f)
        return to == s, local, away

    def hand_over(i):
        rows = tile_rows(i)
        landed(theirs.at[rows], wr_sem.at[i])
        total[rows, :] = (dkv[c, rows, :].astype(F32) + theirs[rows, :].astype(F32)).astype(BF)
        mine, local, away = d_copy(i)

        @pl.when(mine)
        def _():
            local.start()

        @pl.when(jnp.logical_not(mine))
        def _():
            away.start()

    def long_tile(k, carry):
        i = SEQLEN // QT - 1 - k
        attend(i, 5)

        @pl.when(k > 0)
        def _():
            hand_over(i + 1)

        return carry

    lax.fori_loop(0, 4, long_tile, 0)
    for i in (3, 2, 1, 0):
        attend(jnp.int32(i), i + 1)
        hand_over(jnp.int32(i + 1))
        if i == 2:
            cross.wait_recv()
            spread.start()
    hand_over(jnp.int32(0))

    own_head = pl.ds(pl.multiple_of(s * HD, HD), HD)
    own_seq = pl.ds(pl.multiple_of(s * TOK, TOK), TOK)
    keep_o = pltpu.make_async_copy(obuf.at[own_seq], out_ref.at[:, own_head], ol_sem)
    keep_o.start()
    for step in range(1, 2 * NZ):
        to = ring(s + step, 2 * NZ)
        theirs_tok = pl.ds(pl.multiple_of(to * TOK, TOK), TOK)
        remote(
            obuf.at[theirs_tok], out_ref.at[:, own_head], os_sem, or_sem, to, f
        ).start()
    keep_x.wait()
    spread.wait_recv()

    own_tok = pl.ds(pl.multiple_of(e * CTOK, CTOK), CTOK)
    pair_tok = pl.ds(pl.multiple_of((1 - e) * CTOK, CTOK), CTOK)

    def a_cols(b, side):
        return pl.ds(pl.multiple_of((side + 2 * b) * HD, HD), HD)

    def a_copy(b):
        return remote(
            dd.at[b, pair_tok], da.at[:, a_cols(b, e)], as_sem.at[b], ar_sem.at[b], partner, f
        )

    def take_in(kind):
        blocks = got.at[pl.ds(2 * kind, 2)]
        landed(blocks, dr_sem.at[kind])
        for b in range(2 * kind, 2 * kind + 2):
            block = got[b]
            if kind == 0:
                block = rotated(block.astype(F32), cos_ref[...], -sin_ref[...]).astype(BF)
            dd[b] = block

    def trade(kind):
        for b in range(2 * kind, 2 * kind + 2):
            a_copy(b).start()
            da[:, a_cols(b, e)] = dd[b, own_tok, :]

    def chunk(p, part, a):
        for j in range(4):
            cx, cy = (a, j) if part == 0 else (j, a)
            rows = pl.ds(pl.multiple_of((cx * NY + cy) * ROWS, 16), ROWS)
            part_sum[p, part, cx, cy] = (
                jnp.dot(xt[rows, :], dd[2 * p + part, own_tok, :], preferred_element_type=F32)
                + jnp.dot(xp[rows, :], dd[2 * p + part, pair_tok, :], preferred_element_type=F32)
            ).astype(BF)

    def chunk_ref(p, part, a, which):
        if part == 0:
            return part_sum.at[p, part, a, which]
        return part_sum.at[p, part, which, a]

    first_axis = (x, y)
    second_axis = (y, x)

    def neighbour(part, level, d):
        if (part == 0) == (level == 0):
            return ring(x + d, NX) * NY + y
        return x * NY + ring(y + d, NY)

    halves = (pl.ds(0, 2), pl.ds(2, 2))
    full = pl.ds(0, 4)
    dirs = (1, -1)
    sent = []

    def go(src, dst, send, recv, to_f):
        copy = remote(src, dst, send, recv, s, to_f)
        copy.start()
        sent.append(copy)

    def far(p):
        for part in range(2):
            a = ring(first_axis[part] + 2, 4)
            chunk(p, part, a)
            for h, d in enumerate(dirs):
                go(
                    chunk_ref(p, part, a, halves[h]),
                    r1.at[p, part, h],
                    s1_sem.at[p, part, h],
                    r1_sem.at[p, part, h],
                    neighbour(part, 0, d),
                )

    def near(p):
        for part in range(2):
            for d in (1, -1, 0):
                chunk(p, part, ring(first_axis[part] + d, 4))

    def hop(p):
        for h, d in enumerate(dirs):
            for part in range(2):
                a = ring(first_axis[part] + d, 4)
                landed(r1.at[p, part, h], r1_sem.at[p, part, h])
                for k in range(2):
                    j = 2 * h + k
                    idx = (p, part, a, j) if part == 0 else (p, part, j, a)
                    part_sum[idx] = (
                        part_sum[idx].astype(F32) + r1[p, part, h, k].astype(F32)
                    ).astype(BF)
                go(
                    chunk_ref(p, part, a, full),
                    r2.at[p, part, h],
                    s2_sem.at[p, part, h],
                    r2_sem.at[p, part, h],
                    neighbour(part, 0, d),
                )

    def across(p):
        for part in range(2):
            for h in range(2):
                landed(r2.at[p, part, h], r2_sem.at[p, part, h])
            for j in range(4):
                idx = (p, part, x, j) if part == 0 else (p, part, j, y)
                second[p, part, j] = (
                    part_sum[idx].astype(F32)
                    + r2[p, part, 0, j].astype(F32)
                    + r2[p, part, 1, j].astype(F32)
                ).astype(BF)
            for i, d in enumerate((2, 1, -1)):
                go(
                    second.at[p, part, ring(second_axis[part] + d, 4)],
                    r3.at[p, part, i],
                    s3_sem.at[p, part, i],
                    r3_sem.at[p, part, i],
                    neighbour(part, 1, d),
                )

    def z_copy(b):
        to = 2 * (2 * b + e) + c
        return pair != b, remote(third.at[b], zr.at[pair], zs_sem.at[b], zr_sem, to, f)

    def along(p):
        for part in range(2):
            b = 2 * p + part
            acc = second[p, part, second_axis[part]].astype(F32)
            for i in range(3):
                landed(r3.at[p, part, i], r3_sem.at[p, part, i])
                acc = acc + r3[p, part, i].astype(F32)
            third[b] = acc.astype(BF)
            away, copy = z_copy(b)

            @pl.when(away)
            def _():
                copy.start()

    take_in(0)
    far(0)
    near(0)
    take_in(1)
    far(1)
    trade(0)
    trade(1)
    hop(0)
    near(1)
    hop(1)
    across(0)

    for b in range(4):
        landed(da.at[:, a_cols(b, 1 - e)], ar_sem.at[b])

    def input_tile(i, carry):
        rows = pl.ds(pl.multiple_of(i * 256, 256), 256)
        gi[:, rows] = lax.dot_general(da[...], wv[rows, :], NT, preferred_element_type=F32)
        return carry

    lax.fori_loop(0, D // 256, input_tile, 0)
    mine_tok = pl.ds(pl.multiple_of(c * TOK, TOK), TOK)
    sib_tok = pl.ds(pl.multiple_of((1 - c) * TOK, TOK), TOK)
    gsend[...] = gi[sib_tok, :].astype(BF)
    give = remote(gsend, grecv, g_sem.at[0], g_sem.at[1], sib, f)
    give.start()
    along(0)
    across(1)
    give.wait()
    gin_ref[...] = (gi[mine_tok, :] + grecv[...].astype(F32)).astype(BF)
    along(1)
    for copy in sent:
        copy.wait_send()
    cross.wait_send()
    spread.wait_send()
    for b in range(4):
        a_copy(b).wait_send()

    def settle(i, carry):
        swap(i).wait_send()
        mine, _, away = d_copy(i)

        @pl.when(jnp.logical_not(mine))
        def _():
            away.wait_send()

        return carry

    lax.fori_loop(0, SEQLEN // QT, settle, 0)
    keep_o.wait()
    others = obuf.at[pl.ds(0, SEQLEN - TOK)]
    landed(others, os_sem)
    landed(others, or_sem)
    for b in range(4):
        away, copy = z_copy(b)

        @pl.when(away)
        def _():
            copy.wait_send()

    rest = zr.at[pl.ds(1, 3)]
    landed(rest, zr_sem)
    acc = third[pair].astype(F32)
    for step in range(1, 4):
        acc = acc + zr[ring(pair + step, 4)].astype(F32)
    gw_ref[...] = acc


def k3(lengths, qh, gh, kv, xt, xp, wh, cosine, sine):
    dma = pltpu.SemaphoreType.DMA
    return pl.pallas_call(
        k3_kernel,
        out_shape=(
            jax.ShapeDtypeStruct((TOK, 2048), BF),
            jax.ShapeDtypeStruct((TOK, D), BF),
            jax.ShapeDtypeStruct((ROWS, HD), F32),
        ),
        in_specs=[pl.BlockSpec(memory_space=pltpu.SMEM)] + [VM] * 8,
        out_specs=(VM, VM, VM),
        scratch_shapes=[
            pltpu.VMEM((HD, SEQLEN), BF),
            pltpu.VMEM((5, KT, QT), F32),
            pltpu.VMEM((5, KT, QT), BF),
            pltpu.VMEM((SEQLEN, HD), F32),
            pltpu.VMEM((SEQLEN, HD), F32),
            pltpu.VMEM((SEQLEN, HD), BF),
            pltpu.VMEM((2, SEQLEN, HD), BF),
            pltpu.VMEM((SEQLEN, HD), BF),
            pltpu.VMEM((SEQLEN, HD), BF),
            pltpu.VMEM((4, 2 * CTOK, HD), BF),
            pltpu.VMEM((4, 2 * CTOK, HD), BF),
            pltpu.VMEM((CTOK, HALF), BF),
            pltpu.VMEM((D, CTOK), BF),
            pltpu.VMEM((CTOK, D), F32),
            pltpu.VMEM((TOK, D), BF),
            pltpu.VMEM((TOK, D), BF),
            pltpu.VMEM((2, 2, 4, 4, ROWS, HD), BF),
            pltpu.VMEM((2, 2, 2, 2, ROWS, HD), BF),
            pltpu.VMEM((2, 2, 2, 4, ROWS, HD), BF),
            pltpu.VMEM((2, 2, 4, ROWS, HD), BF),
            pltpu.VMEM((2, 2, 3, ROWS, HD), BF),
            pltpu.VMEM((4, ROWS, HD), BF),
            pltpu.VMEM((4, ROWS, HD), BF),
            dma((5,)),
            dma((8,)),
            dma((8,)),
            dma((8,)),
            dma((2,)),
            dma(()),
            dma(()),
            dma(()),
            dma((4,)),
            dma((4,)),
            dma((2,)),
            dma((2, 2, 2)),
            dma((2, 2, 2)),
            dma((2, 2, 2)),
            dma((2, 2, 2)),
            dma((2, 2, 3)),
            dma((2, 2, 3)),
            dma((4,)),
            dma(()),
        ],
        compiler_params=pltpu.CompilerParams(
            collective_id=1, has_side_effects=True, vmem_limit_bytes=32 << 20
        ),
        name="gradients",
    )(lengths, qh, gh, kv, xt, xp, wh, cosine, sine)


def tables(lengths):
    pair = lax.axis_index("seq") // 4
    places = pair * (2 * CTOK) + jnp.arange(2 * CTOK, dtype=jnp.int32)
    order = jnp.arange(NDOC)
    doc_ends = jnp.sum(jnp.where(order[:, None] <= order[None, :], lengths[:, None], 0), axis=0)
    ended = doc_ends[None, :] <= places[:, None]
    within = places - jnp.sum(jnp.where(ended, lengths[None, :], 0), axis=1)
    exponent = jnp.arange(HD // 2, dtype=F32) * (2.0 / HD)
    rate = jnp.power(ROPE_BASE, -exponent)
    angles = within.astype(F32)[:, None] * rate[None, :]
    cosine, sine = jnp.cos(angles), jnp.sin(angles)
    return (
        jnp.concatenate([cosine, cosine], axis=1),
        jnp.concatenate([-sine, sine], axis=1),
    )


def on_device(inputs, queries, w_kv, doc_lengths, grad_out):
    cosine, sine = tables(doc_lengths[0])
    held = [
        pltpu.with_memory_space_constraint(a, pltpu.HBM)
        for a in (inputs[0], queries[0], w_kv, grad_out[0])
    ]
    qh, gh, kv, xt, xp, wh = k1(*held, cosine, sine)
    out, gin, gw = k3(doc_lengths[0], qh, gh, kv, xt, xp, wh, cosine, sine)
    return out[None], gin[None], gw


def solution(mesh):
    in_specs = (
        P("fsdp", "seq", None),
        P("fsdp", "seq", None),
        P("fsdp", None),
        P("fsdp", None),
        P("fsdp", "seq", None),
    )
    out_specs = (P("fsdp", "seq", None), P("fsdp", "seq", None), P("fsdp", "seq"))
    return jax.shard_map(
        on_device, mesh=mesh, in_specs=in_specs, out_specs=out_specs, check_vma=False
    )
```

time: 122 us -> 121 us (level); the launches traced: 121 us -> 121 us
    pallas_call x1 -> x0, Pallas kernels: 13 us -> none  [k2(): pl.pallas_call(k2_kernel, out_shape=(jax.ShapeDtypeStruct((SEQLEN, HD), B...]
    pallas_call x1, Pallas kernels: 48.1 us -> 55.1 us  [k1(): pl.pallas_call(k1_kernel, out_shape=(seq_block, seq_block, jax.ShapeDtype...]
    pallas_call x1, Pallas kernels: 54 us -> 60.4 us  [k3(): pl.pallas_call(k3_kernel, out_shape=(jax.ShapeDtypeStruct((TOK, 2048), BF...]
where the time goes in v4:
time: 121 us
  Pallas kernels  115 us (95%)
  other arithmetic  2.75 us (2%)
  local copies, waits for them, and re-layouts  2.25 us (2%)
    pallas_call x1, Pallas kernels, k3(): pl.pallas_call(k3_kernel, out_shape=(jax.ShapeDtypeStruct((TOK, 2048), BF...  60.4 us
    pallas_call x1, Pallas kernels, k1(): pl.pallas_call(k1_kernel, out_shape=(seq_block, seq_block, jax.ShapeDtype...  55.1 us

profile of v4, /device:TPU:192, one launch (start us, length us, event | category | flops | bytes accessed | tf_op | source)
XLA Modules:
  0.0 121.1 jit_solution(4658677738239867280)
XLA Ops:
  0.6 0.0 copy-start
  0.7 0.8 select_reduce_fusion.1
  1.5 0.7 select_reduce_fusion
  2.2 1.0 fusion
  3.2 0.2 pad_maximum_fusion
  3.4 55.1 %gather_project.1 = (bf16[2048,128]{1,0:T(8,128)(2,1)S(1)}, bf16[2048,128]{1,0:T(8,128)(2,1)S(1)}, bf16[2,2048,128]{2,1,0:T(8,128)(2,1)S(1)}, bf16[2304,256]{1,0...) custom-call(bf16[128,2304]{1,0:T(8,128)(2,1)} %bitcast.11, bf16[128,2048]{1,0:T(8,128)(2,1)} %bitcast.12, ...), custom_call_target="tpu_custom_call" | custom-call | tf_op jit(solution)/shard_map/gather_project/pallas_call | solution.py:333
  58.5 0.0 copy-done
  58.5 60.4 %gradients.1 = (bf16[128,2048]{1,0:T(8,128)(2,1)S(1)}, bf16[128,2304]{1,0:T(8,128)(2,1)S(1)}, f32[144,128]{1,0:T(8,128)S(1)}) custom-call(s32[8]{0:T(128)S(1)} %bitcast.10, bf16[2048,128]{1,0:T(8,128)(2,1)S(1)} %get-tuple-element.12.q_ref, bf16[2048,128]{1,0:T(8,128)(2,1)S(1)} %get-tuple-element.13.g_ref, ...), custom_call_target="tpu_custom_call" | custom-call | tf_op jit(solution)/shard_map/gradients/pallas_call | solution.py:788
  118.9 0.8 copy.11
  119.7 0.8 copy.12
  120.5 0.6 copy.13
  (3 shorter events, 0.0 us)
Async XLA Ops:
  0.6 57.9 %copy-start = (s32[1,8]{1,0:T(1,128)S(1)}, s32[1,8]{1,0:T(1,128)}, u32[]{:S(2)}) copy-start(s32[1,8]{1,0:T(1,128)} %param.8) | copy-start | bytes 100

commit v5 on v4

--- a/solution.py
+++ b/solution.py
@@ -93,15 +93,12 @@
     gh_ref,
     kv_ref,
     xt_ref,
-    xp_ref,
     wg,
     xs,
-    xp,
     proj,
     wl_sem,
     xl_sem,
     xr_sem,
-    xp_sem,
     ws_sem,
     wr_sem,
     ql_sem,
@@ -263,15 +260,6 @@
         head = pl.ds(pl.multiple_of(to * HD, HD), HD)
         for i, (src, dst) in enumerate(((q_ref, qh_ref), (g_ref, gh_ref))):
             remote(src.at[:, head], dst.at[own_seq], qs_sem.at[i], qr_sem.at[i], to, f).start()
-    cross = remote(
-        xs.at[own_tok, pl.ds(0, D // 2)],
-        xp.at[own_tok],
-        xp_sem.at[0],
-        xp_sem.at[1],
-        other_chip(s, z),
-        f,
-    )
-    cross.start()
 
     near_first(0)
     begin(1)
@@ -284,9 +272,6 @@
     finish(0)
     give_x.wait_recv()
     project(0)
-    cross.wait_recv()
-    spread = remote(xp.at[own_tok], xp.at[own_tok], xp_sem.at[2], xp_sem.at[3], sib, f)
-    spread.start()
     rest_second(1)
     finish(1)
     project(1)
@@ -297,15 +282,7 @@
         xt_ref[cols, :] = xs[:, cols].T
         return carry
 
-    def turn_half(i, carry):
-        cols = pl.ds(pl.multiple_of(i * 128, 128), 128)
-        xp_ref[cols, :] = xp[:, cols].T
-        return carry
-
     lax.fori_loop(0, D // 256, turn, 0)
-    spread.wait()
-    cross.wait_send()
-    lax.fori_loop(0, D // 256, turn_half, 0)
     for copy in sends:
         copy.wait_send()
     give_x.wait_send()
@@ -337,19 +314,16 @@
             seq_block,
             jax.ShapeDtypeStruct((2, SEQLEN, HD), BF),
             jax.ShapeDtypeStruct((D, CTOK), BF),
-            jax.ShapeDtypeStruct((D // 2, CTOK), BF),
             jax.ShapeDtypeStruct((D, HALF), BF),
         ),
         in_specs=[HBM, HBM, HBM, HBM, VM, VM],
-        out_specs=(VM, VM, VM, VM, VM, VM),
+        out_specs=(VM, VM, VM, VM, VM),
         scratch_shapes=[
             pltpu.VMEM((CTOK, D), BF),
-            pltpu.VMEM((CTOK, D // 2), BF),
             pltpu.VMEM((8, CTOK, HD), BF),
             dma((8,)),
             dma(()),
             dma((2,)),
-            dma((4,)),
             dma((80,)),
             dma((2, 2, 4, 4, 2)),
             dma((2,)),
@@ -379,7 +353,6 @@
     g_ref,
     kv_ref,
     xt,
-    xp1,
     wv,
     cos_ref,
     sin_ref,
@@ -389,8 +362,9 @@
     vt,
     wbuf,
     tbuf,
-    dk,
-    dv,
+    inv,
+    delt,
+    gs,
     obuf,
     dkv,
     theirs,
@@ -434,40 +408,25 @@
     e = lax.rem(z, 2)
     pair = z // 2
     partner = other_chip(s, z)
-    half_d = D // 2
-    keep_x = pltpu.make_async_copy(xp1, xp.at[pl.ds(0, half_d)], x_sem.at[0])
-    keep_x.start()
     enter(s, f, x, y)
 
     def landed(ref, sem):
         pltpu.make_async_copy(ref, ref, sem).wait()
 
     own_cols = pl.ds(pl.multiple_of(c * TOK, TOK), TOK)
-    cross = remote(
-        xt.at[pl.ds(half_d, half_d), own_cols],
-        xp.at[pl.ds(half_d, half_d), own_cols],
-        x_sem.at[1],
-        x_sem.at[2],
-        partner,
-        f,
-    )
-    cross.start()
-    spread = remote(
-        xp.at[pl.ds(half_d, half_d), own_cols],
-        xp.at[pl.ds(half_d, half_d), own_cols],
-        x_sem.at[3],
-        x_sem.at[4],
-        sib,
-        f,
-    )
+    cross, spread = [], []
+    for h in range(2):
+        rows = pl.ds(h * (D // 2), D // 2)
+        here, there = xt.at[rows, own_cols], xp.at[rows, own_cols]
+        cross.append(remote(here, there, x_sem.at[0, h], x_sem.at[1, h], partner, f))
+        spread.append(remote(there, there, x_sem.at[2, h], x_sem.at[3, h], sib, f))
+        cross[h].start()
 
     ends = []
     so_far = 0
     for i in range(NDOC):
         so_far = so_far + len_ref[i]
         ends.append(so_far)
-    dk[...] = jnp.zeros_like(dk)
-    dv[...] = jnp.zeros_like(dv)
 
     def flip(i, carry):
         rows = pl.ds(pl.multiple_of(i * KT, KT), KT)
@@ -485,7 +444,7 @@
             dkv.at[1 - c, rows], theirs.at[rows], ws_sem.at[i], wr_sem.at[i], sib, f
         )
 
-    def attend(i, n):
+    def forward(i, n):
         base = i * QT
         rows = tile_rows(i)
         pos = base + lax.broadcasted_iota(jnp.int32, (1, QT), 1)
@@ -495,13 +454,12 @@
         low = jnp.maximum(start, pos - (WIN - 1))
         first = i + 1 - n
         qt = q_ref[rows, :]
-        gt = g_ref[rows, :]
         acc = jnp.zeros((HD, QT), F32)
         norm = jnp.zeros((1, QT), F32)
         key = lax.broadcasted_iota(jnp.int32, (KT, QT), 0)
-        spans = [tile_rows(first + j) for j in range(n)]
         for j in range(n):
-            st = lax.dot_general(kv_ref[0, spans[j], :], qt, NT, preferred_element_type=F32)
+            span = tile_rows(first + j)
+            st = lax.dot_general(kv_ref[0, span, :], qt, NT, preferred_element_type=F32)
             squashed = jnp.tanh(st * (SCALE / CAP))
             allowed = key >= low - (first + j) * KT
             if j == n - 1:
@@ -509,23 +467,31 @@
             weight = jnp.where(allowed, jnp.exp2((CAP * LOG2E) * squashed), 0.0)
             short = weight.astype(BF)
             norm = norm + jnp.sum(weight, axis=0, keepdims=True)
-            wbuf[j] = weight * (1.0 - squashed * squashed)
-            tbuf[j] = short
-            acc = acc + jnp.dot(vt[:, spans[j]], short, preferred_element_type=F32)
+            wbuf[first + j, n - 1 - j] = weight * (1.0 - squashed * squashed)
+            tbuf[first + j, n - 1 - j] = short
+            acc = acc + jnp.dot(vt[:, span], short, preferred_element_type=F32)
         inverse = 1.0 / norm
         out_t = (acc * inverse).astype(BF)
         obuf[rows, :] = out_t.T
-        gt_t = gt.astype(F32).T
-        delta = jnp.sum(gt_t * out_t.astype(F32), axis=0, keepdims=True)
-        scaled = (gt_t * inverse).T.astype(BF)
+        gt_t = g_ref[rows, :].astype(F32).T
+        delt[i] = jnp.sum(gt_t * out_t.astype(F32), axis=0, keepdims=True)
+        inv[i] = inverse
+        gs[rows, :] = (gt_t * inverse).T.astype(BF)
+
+    def backward(t, n):
+        span = tile_rows(t)
+        dk = jnp.zeros((KT, HD), F32)
+        dv = jnp.zeros((KT, HD), F32)
         for j in range(n):
-            dprob = lax.dot_general(kv_ref[1, spans[j], :], gt, NT, preferred_element_type=F32)
-            dscore = (wbuf[j] * inverse * (dprob - delta)).astype(BF)
-            dk[spans[j], :] += jnp.dot(dscore, qt, preferred_element_type=F32)
-            dv[spans[j], :] += jnp.dot(tbuf[j], scaled, preferred_element_type=F32)
-        dkv[0, rows, :] = (dk[rows, :] * SCALE).astype(BF)
-        dkv[1, rows, :] = dv[rows, :].astype(BF)
-        swap(i).start()
+            rows = tile_rows(t + j)
+            dprob = lax.dot_general(
+                kv_ref[1, span, :], g_ref[rows, :], NT, preferred_element_type=F32
+            )
+            dscore = (wbuf[t, j] * inv[t + j] * (dprob - delt[t + j])).astype(BF)
+            dk = dk + jnp.dot(dscore, q_ref[rows, :], preferred_element_type=F32)
+            dv = dv + jnp.dot(tbuf[t, j], gs[rows, :], preferred_element_type=F32)
+        dkv[0, span, :] = (dk * SCALE).astype(BF)
+        dkv[1, span, :] = dv.astype(BF)
 
     head_dev = lax.rem(z, 4)
 
@@ -552,36 +518,43 @@
             away.start()
 
     def long_tile(k, carry):
-        i = SEQLEN // QT - 1 - k
-        attend(i, 5)
+        forward(k + 4, 5)
+        return carry
+
+    for i in range(4):
+        forward(jnp.int32(i), i + 1)
+    lax.fori_loop(0, 4, long_tile, 0)
+
+    tiles = SEQLEN // KT
+
+    def key_tile(k, carry):
+        t = ring(z + k, tiles)
+        count = jnp.minimum(tiles - t, 5)
+        for n in range(1, 6):
+
+            @pl.when(count == n)
+            def _():
+                backward(t, n)
+
+        swap(t).start()
 
         @pl.when(k > 0)
         def _():
-            hand_over(i + 1)
+            hand_over(ring(t - 1, tiles))
+
+        for h in range(2):
+
+            @pl.when(k == 4 + 3 * h)
+            def _():
+                cross[h].wait_recv()
+                spread[h].start()
 
         return carry
 
-    lax.fori_loop(0, 4, long_tile, 0)
-    for i in (3, 2, 1, 0):
-        attend(jnp.int32(i), i + 1)
-        hand_over(jnp.int32(i + 1))
-        if i == 2:
-            cross.wait_recv()
-            spread.start()
-    hand_over(jnp.int32(0))
-
-    own_head = pl.ds(pl.multiple_of(s * HD, HD), HD)
-    own_seq = pl.ds(pl.multiple_of(s * TOK, TOK), TOK)
-    keep_o = pltpu.make_async_copy(obuf.at[own_seq], out_ref.at[:, own_head], ol_sem)
-    keep_o.start()
-    for step in range(1, 2 * NZ):
-        to = ring(s + step, 2 * NZ)
-        theirs_tok = pl.ds(pl.multiple_of(to * TOK, TOK), TOK)
-        remote(
-            obuf.at[theirs_tok], out_ref.at[:, own_head], os_sem, or_sem, to, f
-        ).start()
-    keep_x.wait()
-    spread.wait_recv()
+    lax.fori_loop(0, tiles, key_tile, 0)
+    hand_over(ring(z - 1, tiles))
+    for h in range(2):
+        spread[h].wait_recv()
 
     own_tok = pl.ds(pl.multiple_of(e * CTOK, CTOK), CTOK)
     pair_tok = pl.ds(pl.multiple_of((1 - e) * CTOK, CTOK), CTOK)
@@ -722,6 +695,16 @@
     far(1)
     trade(0)
     trade(1)
+    own_head = pl.ds(pl.multiple_of(s * HD, HD), HD)
+    own_seq = pl.ds(pl.multiple_of(s * TOK, TOK), TOK)
+    keep_o = pltpu.make_async_copy(obuf.at[own_seq], out_ref.at[:, own_head], ol_sem)
+    keep_o.start()
+    for step in range(1, 2 * NZ):
+        to = ring(s + step, 2 * NZ)
+        theirs_tok = pl.ds(pl.multiple_of(to * TOK, TOK), TOK)
+        remote(
+            obuf.at[theirs_tok], out_ref.at[:, own_head], os_sem, or_sem, to, f
+        ).start()
     hop(0)
     near(1)
     hop(1)
@@ -748,8 +731,9 @@
     along(1)
     for copy in sent:
         copy.wait_send()
-    cross.wait_send()
-    spread.wait_send()
+    for h in range(2):
+        cross[h].wait_send()
+        spread[h].wait_send()
     for b in range(4):
         a_copy(b).wait_send()
 
@@ -783,7 +767,7 @@
     gw_ref[...] = acc
 
 
-def k3(lengths, qh, gh, kv, xt, xp, wh, cosine, sine):
+def k3(lengths, qh, gh, kv, xt, wh, cosine, sine):
     dma = pltpu.SemaphoreType.DMA
     return pl.pallas_call(
         k3_kernel,
@@ -792,14 +776,15 @@
             jax.ShapeDtypeStruct((TOK, D), BF),
             jax.ShapeDtypeStruct((ROWS, HD), F32),
         ),
-        in_specs=[pl.BlockSpec(memory_space=pltpu.SMEM)] + [VM] * 8,
+        in_specs=[pl.BlockSpec(memory_space=pltpu.SMEM)] + [VM] * 7,
         out_specs=(VM, VM, VM),
         scratch_shapes=[
             pltpu.VMEM((HD, SEQLEN), BF),
-            pltpu.VMEM((5, KT, QT), F32),
-            pltpu.VMEM((5, KT, QT), BF),
-            pltpu.VMEM((SEQLEN, HD), F32),
-            pltpu.VMEM((SEQLEN, HD), F32),
+            pltpu.VMEM((8, 5, KT, QT), F32),
+            pltpu.VMEM((8, 5, KT, QT), BF),
+            pltpu.VMEM((8, 1, QT), F32),
+            pltpu.VMEM((8, 1, QT), F32),
+            pltpu.VMEM((SEQLEN, HD), BF),
             pltpu.VMEM((SEQLEN, HD), BF),
             pltpu.VMEM((2, SEQLEN, HD), BF),
             pltpu.VMEM((SEQLEN, HD), BF),
@@ -818,7 +803,7 @@
             pltpu.VMEM((2, 2, 3, ROWS, HD), BF),
             pltpu.VMEM((4, ROWS, HD), BF),
             pltpu.VMEM((4, ROWS, HD), BF),
-            dma((5,)),
+            dma((4, 2)),
             dma((8,)),
             dma((8,)),
             dma((8,)),
@@ -839,10 +824,10 @@
             dma(()),
         ],
         compiler_params=pltpu.CompilerParams(
-            collective_id=1, has_side_effects=True, vmem_limit_bytes=32 << 20
+            collective_id=1, has_side_effects=True, vmem_limit_bytes=40 << 20
         ),
         name="gradients",
-    )(lengths, qh, gh, kv, xt, xp, wh, cosine, sine)
+    )(lengths, qh, gh, kv, xt, wh, cosine, sine)
 
 
 def tables(lengths):
@@ -868,8 +853,8 @@
         pltpu.with_memory_space_constraint(a, pltpu.HBM)
         for a in (inputs[0], queries[0], w_kv, grad_out[0])
     ]
-    qh, gh, kv, xt, xp, wh = k1(*held, cosine, sine)
-    out, gin, gw = k3(doc_lengths[0], qh, gh, kv, xt, xp, wh, cosine, sine)
+    qh, gh, kv, xt, wh = k1(*held, cosine, sine)
+    out, gin, gw = k3(doc_lengths[0], qh, gh, kv, xt, wh, cosine, sine)
     return out[None], gin[None], gw
 
 

time: 121 us -> 113 us (0.934); the launches traced: 121 us -> 112 us
  Pallas kernels: 115 us -> 106 us
    pallas_call x1, Pallas kernels: 55.1 us -> 48.1 us  [k1(): pl.pallas_call(k1_kernel, out_shape=(seq_block, seq_block, jax.ShapeDtype...]
    pallas_call x1, Pallas kernels: 60.4 us -> 58.1 us  [k3(): pl.pallas_call(k3_kernel, out_shape=(jax.ShapeDtypeStruct((TOK, 2048), BF...]
where the time goes in v5:
time: 113 us; the launch traced here: 112 us
  Pallas kernels  106 us (94%)
  other arithmetic  2.75 us (2%)
  local copies, waits for them, and re-layouts  2.25 us (2%)
    pallas_call x1, Pallas kernels, k3(): pl.pallas_call(k3_kernel, out_shape=(jax.ShapeDtypeStruct((TOK, 2048), BF...  58.1 us
    pallas_call x1, Pallas kernels, k1(): pl.pallas_call(k1_kernel, out_shape=(seq_block, seq_block, jax.ShapeDtype...  48.1 us

profile of v5, /device:TPU:192, one launch (start us, length us, event | category | flops | bytes accessed | tf_op | source)
XLA Modules:
  0.0 111.9 jit_solution(11124343810036039754)
XLA Ops:
  0.6 0.0 copy-start
  0.7 0.8 select_reduce_fusion.1
  1.5 0.7 select_reduce_fusion
  2.2 1.0 fusion
  3.2 0.2 pad_maximum_fusion
  3.4 48.1 %gather_project.1 = (bf16[2048,128]{1,0:T(8,128)(2,1)S(1)}, bf16[2048,128]{1,0:T(8,128)(2,1)S(1)}, bf16[2,2048,128]{2,1,0:T(8,128)(2,1)S(1)}, bf16[2304,256]{1,0:T(8,128)(2,1)S(1)}, bf16[2304,1024]{1,0:T(8,128)(2,1)S(1)}) custom-call(bf16[128,2304]{1,0:T(8,128)(2,1)} %bitcast.11, bf16[128,2048]{1,0:T(8,128)(2,1)} %bitcast.12, bf16[144,2048]{1,0:T(8,128)(2,1)} %w_ref.1, ...), custom_call_target="tpu_custom_call" | custom-call | tf_op jit(solution)/shard_map/gather_project/pallas_call | solution.py:310
  51.5 0.0 copy-done
  51.5 58.1 %gradients.1 = (bf16[128,2048]{1,0:T(8,128)(2,1)S(1)}, bf16[128,2304]{1,0:T(8,128)(2,1)S(1)}, f32[144,128]{1,0:T(8,128)S(1)}) custom-call(s32[8]{0:T(128)S(1)} %bitcast.10, bf16[2048,128]{1,0:T(8,128)(2,1)S(1)} %get-tuple-element.11.q_ref, bf16[2048,128]{1,0:T(8,128)(2,1)S(1)} %get-tuple-element.12.g_ref, ...), custom_call_target="tpu_custom_call" | custom-call | tf_op jit(solution)/shard_map/gradients/pallas_call | solution.py:772
  109.6 0.8 copy.11
  110.4 0.8 copy.12
  111.2 0.6 copy.13
  (3 shorter events, 0.0 us)
Async XLA Ops:
  0.6 50.9 %copy-start = (s32[1,8]{1,0:T(1,128)S(1)}, s32[1,8]{1,0:T(1,128)}, u32[]{:S(2)}) copy-start(s32[1,8]{1,0:T(1,128)} %param.8) | copy-start | bytes 100

commit v6 on v5

--- a/solution.py
+++ b/solution.py
@@ -82,7 +82,7 @@
     return values * cosine + pltpu.roll(values, HD // 2, 1) * sine
 
 
-def k1_kernel(
+def project_part(
     x_ref,
     q_ref,
     w_ref,
@@ -92,13 +92,16 @@
     qh_ref,
     gh_ref,
     kv_ref,
-    xt_ref,
+    xt,
+    xp,
     wg,
     xs,
+    xo,
     proj,
     wl_sem,
     xl_sem,
     xr_sem,
+    xc_sem,
     ws_sem,
     wr_sem,
     ql_sem,
@@ -251,15 +254,25 @@
 
     own_seq = pl.ds(pl.multiple_of(s * TOK, TOK), TOK)
     own_head = pl.ds(pl.multiple_of(s * HD, HD), HD)
-    keep = []
-    for i, (src, dst) in enumerate(((q_ref, qh_ref), (g_ref, gh_ref))):
-        keep.append(pltpu.make_async_copy(src.at[:, own_head], dst.at[own_seq], ql_sem.at[i]))
-        keep[-1].start()
-    for step in range(1, 2 * NZ):
-        to = ring(s + step, 2 * NZ)
-        head = pl.ds(pl.multiple_of(to * HD, HD), HD)
-        for i, (src, dst) in enumerate(((q_ref, qh_ref), (g_ref, gh_ref))):
+
+    def deal(i, src, dst):
+        pltpu.make_async_copy(src.at[:, own_head], dst.at[own_seq], ql_sem.at[i]).start()
+        for step in range(1, 2 * NZ):
+            to = ring(s + step, 2 * NZ)
+            head = pl.ds(pl.multiple_of(to * HD, HD), HD)
             remote(src.at[:, head], dst.at[own_seq], qs_sem.at[i], qr_sem.at[i], to, f).start()
+
+    def dealt(i, src, dst):
+        pltpu.make_async_copy(src.at[:, own_head], dst.at[own_seq], ql_sem.at[i]).wait()
+        others = dst.at[pl.ds(0, SEQLEN - TOK)]
+        pltpu.make_async_copy(others, others, qs_sem.at[i]).wait()
+        pltpu.make_async_copy(others, others, qr_sem.at[i]).wait()
+
+    deal(0, q_ref, qh_ref)
+    cross = remote(
+        xs.at[own_tok], xo.at[own_tok], xc_sem.at[0], xc_sem.at[1], other_chip(s, z), f
+    )
+    cross.start()
 
     near_first(0)
     begin(1)
@@ -275,23 +288,30 @@
     rest_second(1)
     finish(1)
     project(1)
+    deal(1, g_ref, gh_ref)
     share(0)
+    cross.wait_recv()
+    spread = remote(xo.at[own_tok], xo.at[own_tok], xc_sem.at[2], xc_sem.at[3], sib, f)
+    spread.start()
 
     def turn(i, carry):
         cols = pl.ds(pl.multiple_of(i * 256, 256), 256)
-        xt_ref[cols, :] = xs[:, cols].T
+        xt[cols, :] = xs[:, cols].T
         return carry
 
+    def turn_other(i, carry):
+        cols = pl.ds(pl.multiple_of(i * 256, 256), 256)
+        xp[cols, :] = xo[:, cols].T
+        return carry
+
     lax.fori_loop(0, D // 256, turn, 0)
+    spread.wait()
+    lax.fori_loop(0, D // 256, turn_other, 0)
+    cross.wait_send()
     for copy in sends:
         copy.wait_send()
     give_x.wait_send()
-    for copy in keep:
-        copy.wait()
-    for i, dst in enumerate((qh_ref, gh_ref)):
-        others = dst.at[pl.ds(0, SEQLEN - TOK)]
-        pltpu.make_async_copy(others, others, qs_sem.at[i]).wait()
-        pltpu.make_async_copy(others, others, qr_sem.at[i]).wait()
+    dealt(0, q_ref, qh_ref)
     share(1)
     for k in range(8):
         mine, _, away = kv_copy(k)
@@ -302,43 +322,7 @@
 
     for copy in shares:
         copy.wait()
-
-
-def k1(x, q, w, g, cosine, sine):
-    dma = pltpu.SemaphoreType.DMA
-    seq_block = jax.ShapeDtypeStruct((SEQLEN, HD), BF)
-    return pl.pallas_call(
-        k1_kernel,
-        out_shape=(
-            seq_block,
-            seq_block,
-            jax.ShapeDtypeStruct((2, SEQLEN, HD), BF),
-            jax.ShapeDtypeStruct((D, CTOK), BF),
-            jax.ShapeDtypeStruct((D, HALF), BF),
-        ),
-        in_specs=[HBM, HBM, HBM, HBM, VM, VM],
-        out_specs=(VM, VM, VM, VM, VM),
-        scratch_shapes=[
-            pltpu.VMEM((CTOK, D), BF),
-            pltpu.VMEM((8, CTOK, HD), BF),
-            dma((8,)),
-            dma(()),
-            dma((2,)),
-            dma((80,)),
-            dma((2, 2, 4, 4, 2)),
-            dma((2,)),
-            dma((2,)),
-            dma((2,)),
-            dma((8,)),
-            dma((2,)),
-            dma((2,)),
-            dma((2,)),
-        ],
-        compiler_params=pltpu.CompilerParams(
-            collective_id=0, has_side_effects=True, vmem_limit_bytes=16 << 20
-        ),
-        name="gather_project",
-    )(x, q, w, g, cosine, sine)
+    return lambda: dealt(1, g_ref, gh_ref)
 
 
 QT = 256
@@ -347,12 +331,14 @@
 LOG2E = 1.4426950408889634
 
 
-def k3_kernel(
+def gradient_part(
+    wait_g,
     len_ref,
     q_ref,
     g_ref,
     kv_ref,
     xt,
+    xp,
     wv,
     cos_ref,
     sin_ref,
@@ -360,6 +346,7 @@
     gin_ref,
     gw_ref,
     vt,
+    ot,
     wbuf,
     tbuf,
     inv,
@@ -372,7 +359,6 @@
     got,
     dd,
     da,
-    xp,
     gi,
     gsend,
     grecv,
@@ -383,7 +369,6 @@
     r3,
     third,
     zr,
-    x_sem,
     ws_sem,
     wr_sem,
     ds_sem,
@@ -408,19 +393,8 @@
     e = lax.rem(z, 2)
     pair = z // 2
     partner = other_chip(s, z)
-    enter(s, f, x, y)
-
     def landed(ref, sem):
         pltpu.make_async_copy(ref, ref, sem).wait()
-
-    own_cols = pl.ds(pl.multiple_of(c * TOK, TOK), TOK)
-    cross, spread = [], []
-    for h in range(2):
-        rows = pl.ds(h * (D // 2), D // 2)
-        here, there = xt.at[rows, own_cols], xp.at[rows, own_cols]
-        cross.append(remote(here, there, x_sem.at[0, h], x_sem.at[1, h], partner, f))
-        spread.append(remote(there, there, x_sem.at[2, h], x_sem.at[3, h], sib, f))
-        cross[h].start()
 
     ends = []
     so_far = 0
@@ -473,10 +447,15 @@
         inverse = 1.0 / norm
         out_t = (acc * inverse).astype(BF)
         obuf[rows, :] = out_t.T
+        inv[i] = inverse
+        ot[:, rows] = out_t
+
+    def prepare(i, carry):
+        rows = tile_rows(i)
         gt_t = g_ref[rows, :].astype(F32).T
-        delt[i] = jnp.sum(gt_t * out_t.astype(F32), axis=0, keepdims=True)
-        inv[i] = inverse
-        gs[rows, :] = (gt_t * inverse).T.astype(BF)
+        delt[i] = jnp.sum(gt_t * ot[:, rows].astype(F32), axis=0, keepdims=True)
+        gs[rows, :] = (gt_t * inv[i]).T.astype(BF)
+        return carry
 
     def backward(t, n):
         span = tile_rows(t)
@@ -525,6 +504,9 @@
         forward(jnp.int32(i), i + 1)
     lax.fori_loop(0, 4, long_tile, 0)
 
+    wait_g()
+    lax.fori_loop(0, SEQLEN // QT, prepare, 0)
+
     tiles = SEQLEN // KT
 
     def key_tile(k, carry):
@@ -542,19 +524,10 @@
         def _():
             hand_over(ring(t - 1, tiles))
 
-        for h in range(2):
-
-            @pl.when(k == 4 + 3 * h)
-            def _():
-                cross[h].wait_recv()
-                spread[h].start()
-
         return carry
 
     lax.fori_loop(0, tiles, key_tile, 0)
     hand_over(ring(z - 1, tiles))
-    for h in range(2):
-        spread[h].wait_recv()
 
     own_tok = pl.ds(pl.multiple_of(e * CTOK, CTOK), CTOK)
     pair_tok = pl.ds(pl.multiple_of((1 - e) * CTOK, CTOK), CTOK)
@@ -731,9 +704,6 @@
     along(1)
     for copy in sent:
         copy.wait_send()
-    for h in range(2):
-        cross[h].wait_send()
-        spread[h].wait_send()
     for b in range(4):
         a_copy(b).wait_send()
 
@@ -767,18 +737,55 @@
     gw_ref[...] = acc
 
 
-def k3(lengths, qh, gh, kv, xt, wh, cosine, sine):
+def whole_kernel(
+    len_ref, x_ref, q_ref, w_ref, g_ref, cos_ref, sin_ref, out_ref, gin_ref, gw_ref, *scratch
+):
+    qh, gh, kv, xt, xp, wg = scratch[:6]
+    first, second = scratch[:PROJECT_SCRATCH], scratch[PROJECT_SCRATCH:]
+    wait_g = project_part(x_ref, q_ref, w_ref, g_ref, cos_ref, sin_ref, *first)
+    gradient_part(
+        wait_g, len_ref, qh, gh, kv, xt, xp, wg, cos_ref, sin_ref, out_ref, gin_ref, gw_ref, *second
+    )
+
+
+PROJECT_SCRATCH = 22
+
+
+def layer(lengths, x, q, w, g, cosine, sine):
     dma = pltpu.SemaphoreType.DMA
     return pl.pallas_call(
-        k3_kernel,
+        whole_kernel,
         out_shape=(
             jax.ShapeDtypeStruct((TOK, 2048), BF),
             jax.ShapeDtypeStruct((TOK, D), BF),
             jax.ShapeDtypeStruct((ROWS, HD), F32),
         ),
-        in_specs=[pl.BlockSpec(memory_space=pltpu.SMEM)] + [VM] * 7,
+        in_specs=[pl.BlockSpec(memory_space=pltpu.SMEM), HBM, HBM, HBM, HBM, VM, VM],
         out_specs=(VM, VM, VM),
         scratch_shapes=[
+            pltpu.VMEM((SEQLEN, HD), BF),
+            pltpu.VMEM((SEQLEN, HD), BF),
+            pltpu.VMEM((2, SEQLEN, HD), BF),
+            pltpu.VMEM((D, CTOK), BF),
+            pltpu.VMEM((D, CTOK), BF),
+            pltpu.VMEM((D, HALF), BF),
+            pltpu.VMEM((CTOK, D), BF),
+            pltpu.VMEM((CTOK, D), BF),
+            pltpu.VMEM((8, CTOK, HD), BF),
+            dma((8,)),
+            dma(()),
+            dma((2,)),
+            dma((4,)),
+            dma((80,)),
+            dma((2, 2, 4, 4, 2)),
+            dma((2,)),
+            dma((2,)),
+            dma((2,)),
+            dma((8,)),
+            dma((2,)),
+            dma((2,)),
+            dma((2,)),
+            pltpu.VMEM((HD, SEQLEN), BF),
             pltpu.VMEM((HD, SEQLEN), BF),
             pltpu.VMEM((8, 5, KT, QT), F32),
             pltpu.VMEM((8, 5, KT, QT), BF),
@@ -792,7 +799,6 @@
             pltpu.VMEM((4, 2 * CTOK, HD), BF),
             pltpu.VMEM((4, 2 * CTOK, HD), BF),
             pltpu.VMEM((CTOK, HALF), BF),
-            pltpu.VMEM((D, CTOK), BF),
             pltpu.VMEM((CTOK, D), F32),
             pltpu.VMEM((TOK, D), BF),
             pltpu.VMEM((TOK, D), BF),
@@ -803,7 +809,6 @@
             pltpu.VMEM((2, 2, 3, ROWS, HD), BF),
             pltpu.VMEM((4, ROWS, HD), BF),
             pltpu.VMEM((4, ROWS, HD), BF),
-            dma((4, 2)),
             dma((8,)),
             dma((8,)),
             dma((8,)),
@@ -824,10 +829,10 @@
             dma(()),
         ],
         compiler_params=pltpu.CompilerParams(
-            collective_id=1, has_side_effects=True, vmem_limit_bytes=40 << 20
+            collective_id=0, has_side_effects=True, vmem_limit_bytes=50 << 20
         ),
-        name="gradients",
-    )(lengths, qh, gh, kv, xt, wh, cosine, sine)
+        name="layer",
+    )(lengths, x, q, w, g, cosine, sine)
 
 
 def tables(lengths):
@@ -853,8 +858,7 @@
         pltpu.with_memory_space_constraint(a, pltpu.HBM)
         for a in (inputs[0], queries[0], w_kv, grad_out[0])
     ]
-    qh, gh, kv, xt, wh = k1(*held, cosine, sine)
-    out, gin, gw = k3(doc_lengths[0], qh, gh, kv, xt, wh, cosine, sine)
+    out, gin, gw = layer(doc_lengths[0], *held, cosine, sine)
     return out[None], gin[None], gw
 
 

time: 113 us -> 109 us (0.965); the launches traced: 112 us -> 109 us
  Pallas kernels: 106 us -> 104 us
  other arithmetic: 2.75 us -> 1.39 us
    pallas_call x2 -> x1, Pallas kernels: 106 us -> 104 us  [layer(): pl.pallas_call(whole_kernel, out_shape=(jax.ShapeDtypeStruct((TOK, 2048),...]
where the time goes in v6:
time: 109 us
  Pallas kernels  104 us (95%)
  local copies, waits for them, and re-layouts  2.89 us (3%)
  other arithmetic  1.39 us (1%)
    pallas_call x1, Pallas kernels, layer(): pl.pallas_call(whole_kernel, out_shape=(jax.ShapeDtypeStruct((TOK, 2048),...  104 us
    unnamed x5, local copies, waits for them, and re-layouts  2.89 us

profile of v6, /device:TPU:192, one launch (start us, length us, event | category | flops | bytes accessed | tf_op | source)
XLA Modules:
  0.0 109.2 jit_solution(8702157119551532883)
XLA Ops:
  0.6 0.0 copy-start
  0.7 0.6 copy-done
  1.3 0.1 select_reduce_fusion.1
  1.4 0.1 select_reduce_fusion
  1.5 1.0 fusion
  2.5 0.2 pad_maximum_fusion
  2.7 104.3 %layer.1 = (bf16[128,2048]{1,0:T(8,128)(2,1)S(1)}, bf16[128,2304]{1,0:T(8,128)(2,1)S(1)}, f32[144,128]{1,0:T(8,128)S(1)}) custom-call(s32[8]{0:T(128)S(1)} %bitcast.10, bf16[128,2304]{1,0:T(8,128)(2,1)} %bitcast.11, bf16[128,2048]{1,0:T(8,128)(2,1)} %bitcast.12, bf16[144,2048]{1,0:T(8,128)(2,1)} %w_ref.1, bf16[128,2048]{1,0:T(8,128)(2,1)} %bitcast.13, ...), custom_call_target="tpu_custom_call" | custom-call | tf_op jit(solution)/shard_map/layer/pallas_call | solution.py:756
  107.0 0.8 copy.11
  107.8 0.8 copy.12
  108.6 0.6 copy.13
  (3 shorter events, 0.0 us)
Async XLA Ops:
  0.6 0.7 copy-start

commit v7 on v6

--- a/solution.py
+++ b/solution.py
@@ -269,10 +269,7 @@
         pltpu.make_async_copy(others, others, qr_sem.at[i]).wait()
 
     deal(0, q_ref, qh_ref)
-    cross = remote(
-        xs.at[own_tok], xo.at[own_tok], xc_sem.at[0], xc_sem.at[1], other_chip(s, z), f
-    )
-    cross.start()
+    deal(1, g_ref, gh_ref)
 
     near_first(0)
     begin(1)
@@ -288,12 +285,11 @@
     rest_second(1)
     finish(1)
     project(1)
-    deal(1, g_ref, gh_ref)
+    cross = remote(
+        xs.at[own_tok], xo.at[own_tok], xc_sem.at[0], xc_sem.at[1], other_chip(s, z), f
+    )
+    cross.start()
     share(0)
-    cross.wait_recv()
-    spread = remote(xo.at[own_tok], xo.at[own_tok], xc_sem.at[2], xc_sem.at[3], sib, f)
-    spread.start()
-
     def turn(i, carry):
         cols = pl.ds(pl.multiple_of(i * 256, 256), 256)
         xt[cols, :] = xs[:, cols].T
@@ -305,9 +301,6 @@
         return carry
 
     lax.fori_loop(0, D // 256, turn, 0)
-    spread.wait()
-    lax.fori_loop(0, D // 256, turn_other, 0)
-    cross.wait_send()
     for copy in sends:
         copy.wait_send()
     give_x.wait_send()
@@ -322,7 +315,18 @@
 
     for copy in shares:
         copy.wait()
-    return lambda: dealt(1, g_ref, gh_ref)
+    spread = remote(xo.at[own_tok], xo.at[own_tok], xc_sem.at[2], xc_sem.at[3], sib, f)
+
+    def pass_tokens():
+        cross.wait_recv()
+        spread.start()
+
+    def take_tokens():
+        spread.wait()
+        lax.fori_loop(0, D // 256, turn_other, 0)
+        cross.wait_send()
+
+    return lambda: dealt(1, g_ref, gh_ref), pass_tokens, take_tokens
 
 
 QT = 256
@@ -332,7 +336,7 @@
 
 
 def gradient_part(
-    wait_g,
+    waits,
     len_ref,
     q_ref,
     g_ref,
@@ -504,6 +508,7 @@
         forward(jnp.int32(i), i + 1)
     lax.fori_loop(0, 4, long_tile, 0)
 
+    wait_g, pass_tokens, take_tokens = waits
     wait_g()
     lax.fori_loop(0, SEQLEN // QT, prepare, 0)
 
@@ -528,6 +533,8 @@
 
     lax.fori_loop(0, tiles, key_tile, 0)
     hand_over(ring(z - 1, tiles))
+    pass_tokens()
+    take_tokens()
 
     own_tok = pl.ds(pl.multiple_of(e * CTOK, CTOK), CTOK)
     pair_tok = pl.ds(pl.multiple_of((1 - e) * CTOK, CTOK), CTOK)
@@ -742,9 +749,9 @@
 ):
     qh, gh, kv, xt, xp, wg = scratch[:6]
     first, second = scratch[:PROJECT_SCRATCH], scratch[PROJECT_SCRATCH:]
-    wait_g = project_part(x_ref, q_ref, w_ref, g_ref, cos_ref, sin_ref, *first)
+    waits = project_part(x_ref, q_ref, w_ref, g_ref, cos_ref, sin_ref, *first)
     gradient_part(
-        wait_g, len_ref, qh, gh, kv, xt, xp, wg, cos_ref, sin_ref, out_ref, gin_ref, gw_ref, *second
+        waits, len_ref, qh, gh, kv, xt, xp, wg, cos_ref, sin_ref, out_ref, gin_ref, gw_ref, *second
     )
 
 

time: 109 us -> 105 us (0.963)
  Pallas kernels: 104 us -> 99.4 us
    pallas_call x1, Pallas kernels: 104 us -> 99.4 us  [layer(): pl.pallas_call(whole_kernel, out_shape=(jax.ShapeDtypeStruct((TOK, 2048),...]
where the time goes in v7:
time: 105 us; the launch traced here: 104 us
  Pallas kernels  99.4 us (95%)
  local copies, waits for them, and re-layouts  2.89 us (3%)
  other arithmetic  1.39 us (1%)
    pallas_call x1, Pallas kernels, layer(): pl.pallas_call(whole_kernel, out_shape=(jax.ShapeDtypeStruct((TOK, 2048),...  99.4 us
    unnamed x5, local copies, waits for them, and re-layouts  2.89 us

profile of v7, /device:TPU:192, one launch (start us, length us, event | category | flops | bytes accessed | tf_op | source)
XLA Modules:
  0.0 104.4 jit_solution(14224457499427917049)
XLA Ops:
  0.6 0.0 copy-start
  0.7 0.6 copy-done
  1.3 0.1 select_reduce_fusion.1
  1.4 0.1 select_reduce_fusion
  1.5 1.0 fusion
  2.5 0.2 pad_maximum_fusion
  2.7 99.4 %layer.1 = (bf16[128,2048]{1,0:T(8,128)(2,1)S(1)}, bf16[128,2304]{1,0:T(8,128)(2,1)S(1)}, f32[144,128]{1,0:T(8,128)S(1)}) custom-call(s32[8]{0:T(128)S(1)} %bitcast.10, bf16[128,2304]{1,0:T(8,128)(2,1)} %bitcast.11, bf16[128,2048]{1,0:T(8,128)(2,1)} %bitcast.12, bf16[144,2048]{1,0:T(8,128)(2,1)} %w_ref.1, bf16[128,2048]{1,0:T(8,128)(2,1)} %bitcast.13, ...), custom_call_target="tpu_custom_call" | custom-call | tf_op jit(solution)/shard_map/layer/pallas_call | solution.py:763
  102.1 0.8 copy.11
  102.9 0.8 copy.12
  103.7 0.6 copy.13
  (3 shorter events, 0.0 us)
Async XLA Ops:
  0.6 0.7 copy-start

commit v8 on v7

--- a/solution.py
+++ b/solution.py
@@ -534,7 +534,6 @@
     lax.fori_loop(0, tiles, key_tile, 0)
     hand_over(ring(z - 1, tiles))
     pass_tokens()
-    take_tokens()
 
     own_tok = pl.ds(pl.multiple_of(e * CTOK, CTOK), CTOK)
     pair_tok = pl.ds(pl.multiple_of((1 - e) * CTOK, CTOK), CTOK)
@@ -669,12 +668,13 @@
                 copy.start()
 
     take_in(0)
+    trade(0)
+    take_in(1)
+    trade(1)
+    take_tokens()
     far(0)
     near(0)
-    take_in(1)
     far(1)
-    trade(0)
-    trade(1)
     own_head = pl.ds(pl.multiple_of(s * HD, HD), HD)
     own_seq = pl.ds(pl.multiple_of(s * TOK, TOK), TOK)
     keep_o = pltpu.make_async_copy(obuf.at[own_seq], out_ref.at[:, own_head], ol_sem)

time: 105 us -> 105 us (level)
  no operation moved by 1% of the time
where the time goes in v8:
time: 105 us
  Pallas kernels  99.7 us (95%)
  local copies, waits for them, and re-layouts  2.89 us (3%)
  other arithmetic  1.39 us (1%)
    pallas_call x1, Pallas kernels, layer(): pl.pallas_call(whole_kernel, out_shape=(jax.ShapeDtypeStruct((TOK, 2048),...  99.7 us
    unnamed x5, local copies, waits for them, and re-layouts  2.89 us

profile of v8, /device:TPU:192, one launch (start us, length us, event | category | flops | bytes accessed | tf_op | source)
XLA Modules:
  0.0 104.7 jit_solution(3447730072315123453)
XLA Ops:
  0.6 0.0 copy-start
  0.7 0.6 copy-done
  1.3 0.1 select_reduce_fusion.1
  1.4 0.1 select_reduce_fusion
  1.5 1.0 fusion
  2.5 0.2 pad_maximum_fusion
  2.7 99.7 %layer.1 = (bf16[128,2048]{1,0:T(8,128)(2,1)S(1)}, bf16[128,2304]{1,0:T(8,128)(2,1)S(1)}, f32[144,128]{1,0:T(8,128)S(1)}) custom-call(s32[8]{0:T(128)S(1)} %bitcast.10, bf16[128,2304]{1,0:T(8,128)(2,1)} %bitcast.11, bf16[128,2048]{1,0:T(8,128)(2,1)} %bitcast.12, bf16[144,2048]{1,0:T(8,128)(2,1)} %w_ref.1, bf16[128,2048]{1,0:T(8,128)(2,1)} %bitcast.13, ...), custom_call_target="tpu_custom_call" | custom-call | tf_op jit(solution)/shard_map/layer/pallas_call | solution.py:763
  102.4 0.8 copy.11
  103.2 0.8 copy.12
  104.0 0.6 copy.13
  (3 shorter events, 0.0 us)
Async XLA Ops:
  0.6 0.7 copy-start

commit v9 on v8

--- a/solution.py
+++ b/solution.py
@@ -673,8 +673,8 @@
     trade(1)
     take_tokens()
     far(0)
+    far(1)
     near(0)
-    far(1)
     own_head = pl.ds(pl.multiple_of(s * HD, HD), HD)
     own_seq = pl.ds(pl.multiple_of(s * TOK, TOK), TOK)
     keep_o = pltpu.make_async_copy(obuf.at[own_seq], out_ref.at[:, own_head], ol_sem)

time: 105 us -> 105 us (level)
  no operation moved by 1% of the time
where the time goes in v9:
time: 105 us
  Pallas kernels  99.7 us (95%)
  local copies, waits for them, and re-layouts  2.89 us (3%)
  other arithmetic  1.39 us (1%)
    pallas_call x1, Pallas kernels, layer(): pl.pallas_call(whole_kernel, out_shape=(jax.ShapeDtypeStruct((TOK, 2048),...  99.7 us
    unnamed x5, local copies, waits for them, and re-layouts  2.89 us

profile of v9, /device:TPU:192, one launch (start us, length us, event | category | flops | bytes accessed | tf_op | source)
XLA Modules:
  0.0 104.7 jit_solution(17512213306415352179)
XLA Ops:
  0.6 0.0 copy-start
  0.7 0.6 copy-done
  1.3 0.1 select_reduce_fusion.1
  1.4 0.1 select_reduce_fusion
  1.5 1.0 fusion
  2.5 0.2 pad_maximum_fusion
  2.7 99.7 %layer.1 = (bf16[128,2048]{1,0:T(8,128)(2,1)S(1)}, bf16[128,2304]{1,0:T(8,128)(2,1)S(1)}, f32[144,128]{1,0:T(8,128)S(1)}) custom-call(s32[8]{0:T(128)S(1)} %bitcast.10, bf16[128,2304]{1,0:T(8,128)(2,1)} %bitcast.11, bf16[128,2048]{1,0:T(8,128)(2,1)} %bitcast.12, bf16[144,2048]{1,0:T(8,128)(2,1)} %w_ref.1, bf16[128,2048]{1,0:T(8,128)(2,1)} %bitcast.13, ...), custom_call_target="tpu_custom_call" | custom-call | tf_op jit(solution)/shard_map/layer/pallas_call | solution.py:763
  102.4 0.8 copy.11
  103.2 0.8 copy.12
  104.0 0.6 copy.13
  (3 shorter events, 0.0 us)
Async XLA Ops:
  0.6 0.7 copy-start
